TPU v7x, 256 devices: a whole 4x4x8 slice. The times are simulated.
256 devices in a mesh: pipe: 8 (over x, y_hi), dp: 32 (over y_lo, z, core).
Axes of the slice: x: 4, y: 4 (y_hi: 2, y_lo: 2; y = y_hi * 2 + y_lo), z: 8, core: 2. Of those that a mesh axis runs over, the one named last changes fastest.
Arguments:
- tokens: bfloat16 [2, 64, 32, 4096], P(None, 'dp'), may hold values from -6 to 6
- cotangents: bfloat16 [2, 64, 32, 4096], P(None, 'dp'), may hold values from -1.5 to 1.5
- starts: int32 [2, 64, 4], P(None, 'dp'), may hold values from 0 to 31, as said below
- counts: int32 [2, 64], P(None, 'dp'), may hold values from 1 to 4
- layer_gains: bfloat16 [8, 4096], P('pipe', 'dp'), may hold values from 0.5 to 1.5
- first_map: bfloat16 [8, 4096, 128], P('pipe', 'dp'), may hold values from -0.09375 to 0.09375
- second_map: bfloat16 [8, 128, 4096], P('pipe', None, 'dp'), may hold values from -0.5 to 0.5
Outputs:
- gain_grad: float32 [8, 4096], P('pipe', 'dp')
- first_grad: float32 [8, 4096, 128], P('pipe', 'dp')
- second_grad: float32 [8, 128, 4096], P('pipe', None, 'dp')
Inputs may be any that keep to these rules, and one draw needn't show every extreme that they name: `starts`: each row begins with 0 and rises strictly; a micro-batch's documents begin at the first counts entries of its row, the later entries are not used.
All inputs are finite; a program needn't handle non-finite values.
Results may differ from a plain program's by a relative error of at most 0.03.
Values may be sent and summed in bfloat16 or wider, within the bound.
A program may use at most 64 MiB of HBM per device.

v0:
```python
import jax
import jax.numpy as jnp
from jax import lax
from jax.sharding import PartitionSpec as P

HD = 128


def partner(shard, axis, distance):
    return lax.ppermute(shard, axis, [(i, i ^ 1 << distance) for i in range(lax.axis_size(axis))])


def passed_along(value, axis, steps):
    count = lax.axis_size(axis)
    initial, last = (max(0, -steps), min(count, count - steps))
    return lax.ppermute(value, axis, [(source, source + steps) for source in range(initial, last)])


def shortened(shard):

    def short(part):
        return part.astype(jnp.bfloat16) if part.dtype == jnp.float32 else part

    return jax.tree.map(short, shard)


def doc_allowed(row_starts, row_count, length):
    positions = jnp.arange(length, dtype=jnp.int32)
    entries = jnp.arange(row_starts.shape[0], dtype=jnp.int32)
    started = (row_starts[None, :] <= positions[:, None]) & (entries < row_count)[None, :]
    document = jnp.sum(started.astype(jnp.int32), axis=1)
    matched = document[:, None] == document[None, :]
    return matched & (positions[None, :] <= positions[:, None])


def apply_layer(activation, gain_row, first_weight, second_weight, allowed):
    length = activation.shape[0]
    model_width = activation.shape[1]
    widened = activation.astype(jnp.float32)
    factor = lax.rsqrt(jnp.mean(widened * widened, axis=1, keepdims=True) + 1e-05)
    normed = (widened * factor * gain_row).astype(jnp.bfloat16)
    split_heads = normed.reshape(length, model_width // HD, HD)
    scores = (
        jnp.einsum("qhd,khd->hqk", split_heads, split_heads, preferred_element_type=jnp.float32)
        / HD
    )
    weights = jnp.where(allowed[None, :, :], jnp.exp(scores), 0.0)
    probabilities = (weights / jnp.sum(weights, axis=2, keepdims=True)).astype(jnp.bfloat16)
    mixed_heads = jnp.einsum(
        "hqk,khd->qhd", probabilities, split_heads, preferred_element_type=jnp.float32
    )
    mixed_heads = mixed_heads.reshape(length, model_width).astype(jnp.bfloat16)
    reduced = jnp.dot(mixed_heads, first_weight, preferred_element_type=jnp.float32).astype(
        jnp.bfloat16
    )
    return (widened + jnp.dot(reduced, second_weight, preferred_element_type=jnp.float32)).astype(
        jnp.bfloat16
    )


def layer_back(activation, gain_row, first_weight, second_weight, allowed, cotangent):
    _, pullback = jax.vjp(
        lambda act_in, gain_in, first_in, second_in: apply_layer(
            act_in, gain_in, first_in, second_in, allowed
        ),
        activation,
        gain_row,
        first_weight,
        second_weight,
    )
    return pullback(cotangent)


def add_masked(running_sums, gradients, live_flag):
    return tuple(
        (
            current + jnp.where(live_flag, gradient.astype(jnp.float32), 0.0)
            for current, gradient in zip(running_sums, gradients)
        )
    )


def round_parts(running_sums):
    return tuple(
        (lax.optimization_barrier(current.astype(jnp.bfloat16)) for current in running_sums)
    )


def per_device(tokens, cotangents, starts, counts, layer_gains, first_map, second_map):
    sections = lax.axis_size("pipe")
    my_section = lax.axis_index("pipe")
    bit_count = sections.bit_length() - 1
    micro_count = tokens.shape[1]
    length = tokens.shape[2]
    model_width = tokens.shape[3]
    tick_count = sections + micro_count - 1
    allowed_all = jax.vmap(
        jax.vmap(lambda row_starts, row_count: doc_allowed(row_starts, row_count, length))
    )(starts, counts)
    mirrored = (layer_gains, first_map, second_map)
    for bit_number in range(bit_count):
        mirrored = partner((mirrored[0], mirrored[1], mirrored[2]), "pipe", bit_number)
    stacked = (
        jnp.concatenate((layer_gains, mirrored[0]), axis=0),
        jnp.concatenate((first_map, mirrored[1]), axis=0),
        jnp.concatenate((second_map, mirrored[2]), axis=0),
    )
    full_gain, full_first, full_second = (
        lax.all_gather(stacked[0], "dp", axis=1, tiled=True),
        lax.all_gather(stacked[1], "dp", axis=1, tiled=True),
        lax.all_gather(stacked[2], "dp", axis=2, tiled=True),
    )

    def slot_of(index_value):
        live_flag = (index_value >= 0) & (index_value < micro_count)
        return (jnp.clip(index_value, 0, micro_count - 1), live_flag)

    def forward_tick(tick_index, loop_state):
        from_below, from_above, stashed = loop_state
        down_slot, down_live = slot_of(tick_index - my_section)
        up_slot, up_live = slot_of(tick_index - (sections - 1 - my_section))
        down_input = jnp.where(my_section == 0, tokens[0, down_slot], from_below)
        up_input = jnp.where(my_section == sections - 1, tokens[1, up_slot], from_above)
        down_output = apply_layer(
            down_input, full_gain[0], full_first[0], full_second[0], allowed_all[0, down_slot]
        )
        up_output = apply_layer(
            up_input, full_gain[1], full_first[1], full_second[1], allowed_all[1, up_slot]
        )
        stashed = stashed.at[0, down_slot].set(
            jnp.where(down_live, down_input, stashed[0, down_slot])
        )
        stashed = stashed.at[1, up_slot].set(jnp.where(up_live, up_input, stashed[1, up_slot]))
        from_below = passed_along(down_output, "pipe", 1)
        from_above = passed_along(up_output, "pipe", -1)
        return (from_below, from_above, stashed)

    empty_rows = jnp.zeros((length, model_width), jnp.bfloat16)
    empty_stash = jnp.zeros((2, micro_count, length, model_width), jnp.bfloat16)
    _, _, stashed = lax.fori_loop(
        0, tick_count, forward_tick, (empty_rows, empty_rows, empty_stash)
    )
    zero_sums = (
        jnp.zeros((model_width,), jnp.float32),
        jnp.zeros((model_width, first_map.shape[2]), jnp.float32),
        jnp.zeros((second_map.shape[1], model_width), jnp.float32),
    )

    def backward_tick(tick_index, loop_state):
        from_above, from_below, down_sums, up_sums = loop_state
        down_slot, down_live = slot_of(tick_index - (sections - 1 - my_section))
        up_slot, up_live = slot_of(tick_index - my_section)
        down_cot = jnp.where(my_section == sections - 1, cotangents[0, down_slot], from_above)
        up_cot = jnp.where(my_section == 0, cotangents[1, up_slot], from_below)
        down_back = layer_back(
            stashed[0, down_slot],
            full_gain[0],
            full_first[0],
            full_second[0],
            allowed_all[0, down_slot],
            down_cot,
        )
        up_back = layer_back(
            stashed[1, up_slot],
            full_gain[1],
            full_first[1],
            full_second[1],
            allowed_all[1, up_slot],
            up_cot,
        )
        down_sums = add_masked(down_sums, down_back[1:], down_live)
        up_sums = add_masked(up_sums, up_back[1:], up_live)
        from_above = passed_along(down_back[0], "pipe", -1)
        from_below = passed_along(up_back[0], "pipe", 1)
        return (from_above, from_below, down_sums, up_sums)

    _, _, down_sums, up_sums = lax.fori_loop(
        0, tick_count, backward_tick, (empty_rows, empty_rows, zero_sums, zero_sums)
    )
    down_parts = round_parts(down_sums)
    up_parts = round_parts(up_sums)
    received = up_parts
    for bit_number in range(bit_count):
        received = jax.tree.map(
            lambda part, own: part.astype(own.dtype),
            partner(shortened(received), "pipe", bit_number),
            received,
        )
    pair_sums = tuple(
        (
            own_part.astype(jnp.float32) + other_part.astype(jnp.float32)
            for own_part, other_part in zip(down_parts, received)
        )
    )
    gain_total, first_total, second_total = (
        lax.psum_scatter(
            pair_sums[0].astype(jnp.bfloat16), "dp", scatter_dimension=0, tiled=True
        ).astype(jnp.float32),
        lax.psum_scatter(
            pair_sums[1].astype(jnp.bfloat16), "dp", scatter_dimension=0, tiled=True
        ).astype(jnp.float32),
        lax.psum_scatter(
            pair_sums[2].astype(jnp.bfloat16), "dp", scatter_dimension=1, tiled=True
        ).astype(jnp.float32),
    )
    return (gain_total[None], first_total[None], second_total[None])


def solution(mesh):
    in_specs = (
        P(None, "dp", None, None),
        P(None, "dp", None, None),
        P(None, "dp", None),
        P(None, "dp"),
        P("pipe", "dp"),
        P("pipe", "dp", None),
        P("pipe", None, "dp"),
    )
    out_specs = (P("pipe", "dp"), P("pipe", "dp", None), P("pipe", None, "dp"))
    return jax.shard_map(
        per_device, mesh=mesh, in_specs=in_specs, out_specs=out_specs, check_vma=False
    )
```

profile of v0, /device:TPU:64, one launch (start us, length us, event | category | flops | bytes accessed | tf_op | source)
XLA Modules:
  0.0 1084.1 jit_solution(12410242168434772746)
XLA Ops:
  54.8 33.5 %all_gather.11 = bf16[2,4096]{1,0:T(2,128)(2,1)S(1)} all-gather(bf16[2,128]{1,0:T(2,128)(2,1)S(1)} %pad_maximum_fusion.2), channel_id=1, replica_groups=mesh['pipe'=8,'dp'=32] {'dp'}, dimensions={1}, use_global_device_ids=true | all-gather | bytes 16896 | tf_op jit(solution)/shard_map/all_gather | solution.py:109
  89.9 66.1 %all-gather.5.cloned.1.call-done = bf16[2,4096,128]{2,1,0:T(8,128)(2,1)} async-done(((bf16[2,128,128]{2,1,0:T(8,128)(2,1)}), bf16[2,4096,128]{2,1,0:T(8,128)(2,1)}) %all-gather.5.cloned.1.call-update) | async-done | bytes 2097168 | tf_op jit(solution)/shard_map/all_gather | solution.py:110
  156.9 277.2 %while.49 = (s32[]{:T(128)}, bf16[32,4096]{1,0:T(8,128)(2,1)S(1)}, bf16[32,4096]{1,0:T(8,128)(2,1)}, bf16[2,2,32,4096]{3,2,1,0:T(8,128)(2,1)S(1)}, pred[]{:T(512...) while((s32[]{:T(128)}, bf16[32,4096]{1,0:T(8,128)(2,1)S(1)}, ...), condition=%wide.region_8.9_spmd, body=%wide.region_1.8_spmd.sunk | while | flops 172771520 | bytes 23715560 | solution.py:140
  176.1 6.1 collective-permute-start
  182.2 5.9 collective-permute-done
  207.4 6.4 collective-permute-start
  213.8 5.1 collective-permute-done
  238.1 7.3 collective-permute-start
  245.5 4.2 collective-permute-done
  268.9 7.3 collective-permute-start
  276.3 4.2 collective-permute-done
  299.7 7.3 collective-permute-start
  307.0 4.2 collective-permute-done
  330.4 7.3 collective-permute-start
  337.7 4.2 collective-permute-done
  361.1 7.3 collective-permute-start
  368.5 4.2 collective-permute-done
  391.8 7.3 collective-permute-start
  399.2 4.2 collective-permute-done
  422.6 7.3 collective-permute-start
  429.9 4.2 collective-permute-done
  435.5 326.4 %while.50 = (s32[]{:T(128)}, bf16[32,4096]{1,0:T(8,128)(2,1)}, bf16[32,4096]{1,0:T(8,128)(2,1)}, f32[4096]{0:T(1024)S(1)}, f32[4096,128]{1,0:T(8,128)}, /*index=...) while((s32[]{:T(128)}, bf16[32,4096]{1,0:T(8,128)(2,1)}, ...), condition=%wide.region_20.21_spmd.clone, body=%wide.region_9.20_spmd.clone.sunk | while | flops 456771968 | bytes 73035120 | solution.py:177
  447.1 8.1 collective-permute-start.3
  481.7 7.4 collective-permute-start.3
  518.5 7.0 collective-permute-start.3
  528.6 3.9 fusion.335
  554.9 7.0 collective-permute-start.3
  565.1 3.9 fusion.335
  591.4 7.0 collective-permute-start.3
  601.5 3.9 fusion.335
  627.8 7.0 collective-permute-start.3
  638.0 3.9 fusion.335
  664.3 7.0 collective-permute-start.3
  700.7 7.0 collective-permute-start.3
  710.9 3.9 fusion.335
  737.2 7.0 collective-permute-start.3
  747.3 3.9 fusion.335
  767.7 15.8 %collective-permute-done.19 = bf16[128,4096]{1,0:T(8,128)(2,1)S(1)} collective-permute-done((bf16[128,4096]{1,0:T(8,128)(2,1)S(1)}, bf16[128,4096]{1,0:T(8,128)(2,1)S(1)}, u32[]{:S(2)}, u32[]{:S(2)}) %collective-permute-start.19) | collective-permute-done | bytes 1048608 | tf_op jit(solution)/shard_map/ppermute | solution.py:10
  783.5 7.9 collective-permute-start.20
  791.4 4.0 collective-permute-start.16
  795.5 19.9 %collective-permute-done.20 = bf16[128,4096]{1,0:T(8,128)(2,1)S(1)} collective-permute-done((bf16[128,4096]{1,0:T(8,128)(2,1)S(1)}, bf16[128,4096]{1,0:T(8,128)(2,1)S(1)}, u32[]{:S(2)}, u32[]{:S(2)}) %collective-permute-start.20) | collective-permute-done | bytes 1048608 | tf_op jit(solution)/shard_map/ppermute | solution.py:10
  815.3 8.2 collective-permute-start.21
  825.2 20.7 %collective-permute-done.21 = bf16[128,4096]{1,0:T(8,128)(2,1)S(1)} collective-permute-done((bf16[128,4096]{1,0:T(8,128)(2,1)S(1)}, bf16[128,4096]{1,0:T(8,128)(2,1)S(1)}, u32[]{:S(2)}, u32[]{:S(2)}) %collective-permute-start.21) | collective-permute-done | bytes 1048608 | tf_op jit(solution)/shard_map/ppermute | solution.py:10
  849.7 10.7 collective-permute-done.17
  861.2 15.8 %collective-permute-done.18 = bf16[4096,128]{1,0:T(8,128)(2,1)S(1)} collective-permute-done((bf16[4096,128]{1,0:T(8,128)(2,1)}, bf16[4096,128]{1,0:T(8,128)(2,1)S(1)}, u32[]{:S(2)}, u32[]{:S(2)}) %collective-permute-start.18) | collective-permute-done | bytes 1048608 | tf_op jit(solution)/shard_map/ppermute | solution.py:10
  892.3 46.6 %all-reduce = bf16[4096]{0:T(1024)(128)(2,1)S(1)} all-reduce(bf16[4096]{0:T(1024)(128)(2,1)S(1)} %add_convert_fusion.2), channel_id=2, replica_groups=mesh['pipe'=8,'dp'=32] {'dp'}, use_global_device_ids=true, to_apply=%region_21.22.clone | all-reduce | flops 4096 | bytes 16384
  939.5 20.6 %reduce-scatter.7.cloned.1.call-done = bf16[128,128]{1,0:T(8,128)(2,1)} async-done(((bf16[4096,128]{1,0:T(8,128)(2,1)}), bf16[128,128]{1,0:T(8,128)(2,1)}) %reduce-scatter.7.cloned.1.call-update) | async-done | bytes 32784
  961.6 114.6 %reduce-scatter.5.cloned.1.call-done = bf16[128,128]{1,0:T(8,128)(2,1)} async-done(((bf16[4096,128]{1,0:T(8,128)(2,1)}), bf16[128,128]{1,0:T(8,128)(2,1)}) %reduce-scatter.5.cloned.1.call-update) | async-done | bytes 32784 | tf_op jit(solution)/shard_map/reduce_scatter | solution.py:199
  (783 shorter events, 490.0 us)
Async XLA Ops:
  7.2 82.8 %all-gather.3.cloned.1.call-start = ((), (), s32[]{:S(2)}) async-start(), calls=%async_computation.2 | async-start | bytes 2162688 | tf_op jit(solution)/shard_map/all_gather | solution.py:111
  7.2 5.7 collective-permute-start.4
  23.7 132.3 %all-gather.5.cloned.1.call-start = ((), (), s32[]{:S(2)}) async-start(), calls=%async_computation.3 | async-start | bytes 2162688 | tf_op jit(solution)/shard_map/all_gather | solution.py:110
  23.7 5.7 collective-permute-start.7
  40.2 919.9 %reduce-scatter.7.cloned.1.call-start = ((), (), s32[]{:S(2)}) async-start(), calls=%async_computation.5 | async-start | bytes 1081344
  168.7 13.5 %collective-permute-start.1 = (bf16[32,4096]{1,0:T(8,128)(2,1)}, bf16[32,4096]{1,0:T(8,128)(2,1)}, u32[]{:S(2)}, u32[]{:S(2)}) collective-permute-start(bf16[32,4096]{1,0:T(8,128)(2,1)} %fusion.286), channel_id=1, source_target_pairs={{32,0},{64,32},{96,64},{128,96},{160,128},{192,160},{224,192},{33,... | collective-permute-start | bytes 786440 | tf_op jit(solution)/shard_map/while/body/eval_jaxpr/ppermute | solution.py:16
  176.1 12.0 %collective-permute-start = (bf16[32,4096]{1,0:T(8,128)(2,1)}, bf16[32,4096]{1,0:T(8,128)(2,1)S(1)}, u32[]{:S(2)}, u32[]{:S(2)}) collective-permute-start(bf16[32,4096]{1,0:T(8,128)(2,1)} %fusion.281), channel_id=1, source_target_pairs={{0,32},{32,64},{64,96},{96,128},{128,160},{160,192},{192,224},{1,3... | collective-permute-start | bytes 786440 | tf_op jit(solution)/shard_map/while/body/eval_jaxpr/ppermute | solution.py:16
  200.0 13.8 %collective-permute-start.1 = (bf16[32,4096]{1,0:T(8,128)(2,1)}, bf16[32,4096]{1,0:T(8,128)(2,1)}, u32[]{:S(2)}, u32[]{:S(2)}) collective-permute-start(bf16[32,4096]{1,0:T(8,128)(2,1)} %fusion.286), channel_id=1, source_target_pairs={{32,0},{64,32},{96,64},{128,96},{160,128},{192,160},{224,192},{33,... | collective-permute-start | bytes 786440 | tf_op jit(solution)/shard_map/while/body/eval_jaxpr/ppermute | solution.py:16
  207.4 11.5 %collective-permute-start = (bf16[32,4096]{1,0:T(8,128)(2,1)}, bf16[32,4096]{1,0:T(8,128)(2,1)S(1)}, u32[]{:S(2)}, u32[]{:S(2)}) collective-permute-start(bf16[32,4096]{1,0:T(8,128)(2,1)} %fusion.281), channel_id=1, source_target_pairs={{0,32},{32,64},{64,96},{96,128},{128,160},{160,192},{192,224},{1,3... | collective-permute-start | bytes 786440 | tf_op jit(solution)/shard_map/while/body/eval_jaxpr/ppermute | solution.py:16
  230.7 14.7 %collective-permute-start.1 = (bf16[32,4096]{1,0:T(8,128)(2,1)}, bf16[32,4096]{1,0:T(8,128)(2,1)}, u32[]{:S(2)}, u32[]{:S(2)}) collective-permute-start(bf16[32,4096]{1,0:T(8,128)(2,1)} %fusion.286), channel_id=1, source_target_pairs={{32,0},{64,32},{96,64},{128,96},{160,128},{192,160},{224,192},{33,... | collective-permute-start | bytes 786440 | tf_op jit(solution)/shard_map/while/body/eval_jaxpr/ppermute | solution.py:16
  238.1 11.6 %collective-permute-start = (bf16[32,4096]{1,0:T(8,128)(2,1)}, bf16[32,4096]{1,0:T(8,128)(2,1)S(1)}, u32[]{:S(2)}, u32[]{:S(2)}) collective-permute-start(bf16[32,4096]{1,0:T(8,128)(2,1)} %fusion.281), channel_id=1, source_target_pairs={{0,32},{32,64},{64,96},{96,128},{128,160},{160,192},{192,224},{1,3... | collective-permute-start | bytes 786440 | tf_op jit(solution)/shard_map/while/body/eval_jaxpr/ppermute | solution.py:16
  261.5 14.7 %collective-permute-start.1 = (bf16[32,4096]{1,0:T(8,128)(2,1)}, bf16[32,4096]{1,0:T(8,128)(2,1)}, u32[]{:S(2)}, u32[]{:S(2)}) collective-permute-start(bf16[32,4096]{1,0:T(8,128)(2,1)} %fusion.286), channel_id=1, source_target_pairs={{32,0},{64,32},{96,64},{128,96},{160,128},{192,160},{224,192},{33,... | collective-permute-start | bytes 786440 | tf_op jit(solution)/shard_map/while/body/eval_jaxpr/ppermute | solution.py:16
  268.9 11.5 %collective-permute-start = (bf16[32,4096]{1,0:T(8,128)(2,1)}, bf16[32,4096]{1,0:T(8,128)(2,1)S(1)}, u32[]{:S(2)}, u32[]{:S(2)}) collective-permute-start(bf16[32,4096]{1,0:T(8,128)(2,1)} %fusion.281), channel_id=1, source_target_pairs={{0,32},{32,64},{64,96},{96,128},{128,160},{160,192},{192,224},{1,3... | collective-permute-start | bytes 786440 | tf_op jit(solution)/shard_map/while/body/eval_jaxpr/ppermute | solution.py:16
  292.3 14.7 %collective-permute-start.1 = (bf16[32,4096]{1,0:T(8,128)(2,1)}, bf16[32,4096]{1,0:T(8,128)(2,1)}, u32[]{:S(2)}, u32[]{:S(2)}) collective-permute-start(bf16[32,4096]{1,0:T(8,128)(2,1)} %fusion.286), channel_id=1, source_target_pairs={{32,0},{64,32},{96,64},{128,96},{160,128},{192,160},{224,192},{33,... | collective-permute-start | bytes 786440 | tf_op jit(solution)/shard_map/while/body/eval_jaxpr/ppermute | solution.py:16
  299.7 11.5 %collective-permute-start = (bf16[32,4096]{1,0:T(8,128)(2,1)}, bf16[32,4096]{1,0:T(8,128)(2,1)S(1)}, u32[]{:S(2)}, u32[]{:S(2)}) collective-permute-start(bf16[32,4096]{1,0:T(8,128)(2,1)} %fusion.281), channel_id=1, source_target_pairs={{0,32},{32,64},{64,96},{96,128},{128,160},{160,192},{192,224},{1,3... | collective-permute-start | bytes 786440 | tf_op jit(solution)/shard_map/while/body/eval_jaxpr/ppermute | solution.py:16
  323.0 14.7 %collective-permute-start.1 = (bf16[32,4096]{1,0:T(8,128)(2,1)}, bf16[32,4096]{1,0:T(8,128)(2,1)}, u32[]{:S(2)}, u32[]{:S(2)}) collective-permute-start(bf16[32,4096]{1,0:T(8,128)(2,1)} %fusion.286), channel_id=1, source_target_pairs={{32,0},{64,32},{96,64},{128,96},{160,128},{192,160},{224,192},{33,... | collective-permute-start | bytes 786440 | tf_op jit(solution)/shard_map/while/body/eval_jaxpr/ppermute | solution.py:16
  330.4 11.5 %collective-permute-start = (bf16[32,4096]{1,0:T(8,128)(2,1)}, bf16[32,4096]{1,0:T(8,128)(2,1)S(1)}, u32[]{:S(2)}, u32[]{:S(2)}) collective-permute-start(bf16[32,4096]{1,0:T(8,128)(2,1)} %fusion.281), channel_id=1, source_target_pairs={{0,32},{32,64},{64,96},{96,128},{128,160},{160,192},{192,224},{1,3... | collective-permute-start | bytes 786440 | tf_op jit(solution)/shard_map/while/body/eval_jaxpr/ppermute | solution.py:16
  353.7 14.7 %collective-permute-start.1 = (bf16[32,4096]{1,0:T(8,128)(2,1)}, bf16[32,4096]{1,0:T(8,128)(2,1)}, u32[]{:S(2)}, u32[]{:S(2)}) collective-permute-start(bf16[32,4096]{1,0:T(8,128)(2,1)} %fusion.286), channel_id=1, source_target_pairs={{32,0},{64,32},{96,64},{128,96},{160,128},{192,160},{224,192},{33,... | collective-permute-start | bytes 786440 | tf_op jit(solution)/shard_map/while/body/eval_jaxpr/ppermute | solution.py:16
  361.1 11.5 %collective-permute-start = (bf16[32,4096]{1,0:T(8,128)(2,1)}, bf16[32,4096]{1,0:T(8,128)(2,1)S(1)}, u32[]{:S(2)}, u32[]{:S(2)}) collective-permute-start(bf16[32,4096]{1,0:T(8,128)(2,1)} %fusion.281), channel_id=1, source_target_pairs={{0,32},{32,64},{64,96},{96,128},{128,160},{160,192},{192,224},{1,3... | collective-permute-start | bytes 786440 | tf_op jit(solution)/shard_map/while/body/eval_jaxpr/ppermute | solution.py:16
  384.4 14.7 %collective-permute-start.1 = (bf16[32,4096]{1,0:T(8,128)(2,1)}, bf16[32,4096]{1,0:T(8,128)(2,1)}, u32[]{:S(2)}, u32[]{:S(2)}) collective-permute-start(bf16[32,4096]{1,0:T(8,128)(2,1)} %fusion.286), channel_id=1, source_target_pairs={{32,0},{64,32},{96,64},{128,96},{160,128},{192,160},{224,192},{33,... | collective-permute-start | bytes 786440 | tf_op jit(solution)/shard_map/while/body/eval_jaxpr/ppermute | solution.py:16
  391.8 11.5 %collective-permute-start = (bf16[32,4096]{1,0:T(8,128)(2,1)}, bf16[32,4096]{1,0:T(8,128)(2,1)S(1)}, u32[]{:S(2)}, u32[]{:S(2)}) collective-permute-start(bf16[32,4096]{1,0:T(8,128)(2,1)} %fusion.281), channel_id=1, source_target_pairs={{0,32},{32,64},{64,96},{96,128},{128,160},{160,192},{192,224},{1,3... | collective-permute-start | bytes 786440 | tf_op jit(solution)/shard_map/while/body/eval_jaxpr/ppermute | solution.py:16
  415.2 14.7 %collective-permute-start.1 = (bf16[32,4096]{1,0:T(8,128)(2,1)}, bf16[32,4096]{1,0:T(8,128)(2,1)}, u32[]{:S(2)}, u32[]{:S(2)}) collective-permute-start(bf16[32,4096]{1,0:T(8,128)(2,1)} %fusion.286), channel_id=1, source_target_pairs={{32,0},{64,32},{96,64},{128,96},{160,128},{192,160},{224,192},{33,... | collective-permute-start | bytes 786440 | tf_op jit(solution)/shard_map/while/body/eval_jaxpr/ppermute | solution.py:16
  422.6 11.5 %collective-permute-start = (bf16[32,4096]{1,0:T(8,128)(2,1)}, bf16[32,4096]{1,0:T(8,128)(2,1)S(1)}, u32[]{:S(2)}, u32[]{:S(2)}) collective-permute-start(bf16[32,4096]{1,0:T(8,128)(2,1)} %fusion.281), channel_id=1, source_target_pairs={{0,32},{32,64},{64,96},{96,128},{128,160},{160,192},{192,224},{1,3... | collective-permute-start | bytes 786440 | tf_op jit(solution)/shard_map/while/body/eval_jaxpr/ppermute | solution.py:16
  445.9 24.1 %collective-permute-start.2 = (bf16[32,4096]{1,0:T(8,128)(2,1)}, bf16[32,4096]{1,0:T(8,128)(2,1)}, u32[]{:S(2)}, u32[]{:S(2)}) collective-permute-start(bf16[32,4096]{1,0:T(8,128)(2,1)} %fusion.332), channel_id=1, source_target_pairs={{32,0},{64,32},{96,64},{128,96},{160,128},{192,160},{224,192},{33,... | collective-permute-start | bytes 786440 | tf_op jit(solution)/shard_map/while/body/eval_jaxpr/ppermute | solution.py:16
  447.1 22.9 %collective-permute-start.3 = (bf16[32,4096]{1,0:T(8,128)(2,1)}, bf16[32,4096]{1,0:T(8,128)(2,1)}, u32[]{:S(2)}, u32[]{:S(2)}) collective-permute-start(bf16[32,4096]{1,0:T(8,128)(2,1)} %get-tuple-element.1028), channel_id=1, source_target_pairs={{0,32},{32,64},{64,96},{96,128},{128,160},{160,192},{192,224},{1,3... | collective-permute-start | bytes 786440 | tf_op jit(solution)/shard_map/while/body/eval_jaxpr/ppermute | solution.py:16
  480.4 26.4 %collective-permute-start.2 = (bf16[32,4096]{1,0:T(8,128)(2,1)}, bf16[32,4096]{1,0:T(8,128)(2,1)}, u32[]{:S(2)}, u32[]{:S(2)}) collective-permute-start(bf16[32,4096]{1,0:T(8,128)(2,1)} %fusion.332), channel_id=1, source_target_pairs={{32,0},{64,32},{96,64},{128,96},{160,128},{192,160},{224,192},{33,... | collective-permute-start | bytes 786440 | tf_op jit(solution)/shard_map/while/body/eval_jaxpr/ppermute | solution.py:16
  481.7 25.1 %collective-permute-start.3 = (bf16[32,4096]{1,0:T(8,128)(2,1)}, bf16[32,4096]{1,0:T(8,128)(2,1)}, u32[]{:S(2)}, u32[]{:S(2)}) collective-permute-start(bf16[32,4096]{1,0:T(8,128)(2,1)} %get-tuple-element.1028), channel_id=1, source_target_pairs={{0,32},{32,64},{64,96},{96,128},{128,160},{160,192},{192,224},{1,3... | collective-permute-start | bytes 786440 | tf_op jit(solution)/shard_map/while/body/eval_jaxpr/ppermute | solution.py:16
  517.2 26.0 %collective-permute-start.2 = (bf16[32,4096]{1,0:T(8,128)(2,1)}, bf16[32,4096]{1,0:T(8,128)(2,1)}, u32[]{:S(2)}, u32[]{:S(2)}) collective-permute-start(bf16[32,4096]{1,0:T(8,128)(2,1)} %fusion.332), channel_id=1, source_target_pairs={{32,0},{64,32},{96,64},{128,96},{160,128},{192,160},{224,192},{33,... | collective-permute-start | bytes 786440 | tf_op jit(solution)/shard_map/while/body/eval_jaxpr/ppermute | solution.py:16
  518.5 24.8 %collective-permute-start.3 = (bf16[32,4096]{1,0:T(8,128)(2,1)}, bf16[32,4096]{1,0:T(8,128)(2,1)}, u32[]{:S(2)}, u32[]{:S(2)}) collective-permute-start(bf16[32,4096]{1,0:T(8,128)(2,1)} %get-tuple-element.1028), channel_id=1, source_target_pairs={{0,32},{32,64},{64,96},{96,128},{128,160},{160,192},{192,224},{1,3... | collective-permute-start | bytes 786440 | tf_op jit(solution)/shard_map/while/body/eval_jaxpr/ppermute | solution.py:16
  553.7 26.0 %collective-permute-start.2 = (bf16[32,4096]{1,0:T(8,128)(2,1)}, bf16[32,4096]{1,0:T(8,128)(2,1)}, u32[]{:S(2)}, u32[]{:S(2)}) collective-permute-start(bf16[32,4096]{1,0:T(8,128)(2,1)} %fusion.332), channel_id=1, source_target_pairs={{32,0},{64,32},{96,64},{128,96},{160,128},{192,160},{224,192},{33,... | collective-permute-start | bytes 786440 | tf_op jit(solution)/shard_map/while/body/eval_jaxpr/ppermute | solution.py:16
  554.9 24.8 %collective-permute-start.3 = (bf16[32,4096]{1,0:T(8,128)(2,1)}, bf16[32,4096]{1,0:T(8,128)(2,1)}, u32[]{:S(2)}, u32[]{:S(2)}) collective-permute-start(bf16[32,4096]{1,0:T(8,128)(2,1)} %get-tuple-element.1028), channel_id=1, source_target_pairs={{0,32},{32,64},{64,96},{96,128},{128,160},{160,192},{192,224},{1,3... | collective-permute-start | bytes 786440 | tf_op jit(solution)/shard_map/while/body/eval_jaxpr/ppermute | solution.py:16
  590.1 26.0 %collective-permute-start.2 = (bf16[32,4096]{1,0:T(8,128)(2,1)}, bf16[32,4096]{1,0:T(8,128)(2,1)}, u32[]{:S(2)}, u32[]{:S(2)}) collective-permute-start(bf16[32,4096]{1,0:T(8,128)(2,1)} %fusion.332), channel_id=1, source_target_pairs={{32,0},{64,32},{96,64},{128,96},{160,128},{192,160},{224,192},{33,... | collective-permute-start | bytes 786440 | tf_op jit(solution)/shard_map/while/body/eval_jaxpr/ppermute | solution.py:16
  591.4 24.8 %collective-permute-start.3 = (bf16[32,4096]{1,0:T(8,128)(2,1)}, bf16[32,4096]{1,0:T(8,128)(2,1)}, u32[]{:S(2)}, u32[]{:S(2)}) collective-permute-start(bf16[32,4096]{1,0:T(8,128)(2,1)} %get-tuple-element.1028), channel_id=1, source_target_pairs={{0,32},{32,64},{64,96},{96,128},{128,160},{160,192},{192,224},{1,3... | collective-permute-start | bytes 786440 | tf_op jit(solution)/shard_map/while/body/eval_jaxpr/ppermute | solution.py:16
  626.5 26.0 %collective-permute-start.2 = (bf16[32,4096]{1,0:T(8,128)(2,1)}, bf16[32,4096]{1,0:T(8,128)(2,1)}, u32[]{:S(2)}, u32[]{:S(2)}) collective-permute-start(bf16[32,4096]{1,0:T(8,128)(2,1)} %fusion.332), channel_id=1, source_target_pairs={{32,0},{64,32},{96,64},{128,96},{160,128},{192,160},{224,192},{33,... | collective-permute-start | bytes 786440 | tf_op jit(solution)/shard_map/while/body/eval_jaxpr/ppermute | solution.py:16
  627.8 24.8 %collective-permute-start.3 = (bf16[32,4096]{1,0:T(8,128)(2,1)}, bf16[32,4096]{1,0:T(8,128)(2,1)}, u32[]{:S(2)}, u32[]{:S(2)}) collective-permute-start(bf16[32,4096]{1,0:T(8,128)(2,1)} %get-tuple-element.1028), channel_id=1, source_target_pairs={{0,32},{32,64},{64,96},{96,128},{128,160},{160,192},{192,224},{1,3... | collective-permute-start | bytes 786440 | tf_op jit(solution)/shard_map/while/body/eval_jaxpr/ppermute | solution.py:16
  663.0 26.0 %collective-permute-start.2 = (bf16[32,4096]{1,0:T(8,128)(2,1)}, bf16[32,4096]{1,0:T(8,128)(2,1)}, u32[]{:S(2)}, u32[]{:S(2)}) collective-permute-start(bf16[32,4096]{1,0:T(8,128)(2,1)} %fusion.332), channel_id=1, source_target_pairs={{32,0},{64,32},{96,64},{128,96},{160,128},{192,160},{224,192},{33,... | collective-permute-start | bytes 786440 | tf_op jit(solution)/shard_map/while/body/eval_jaxpr/ppermute | solution.py:16
  664.3 24.8 %collective-permute-start.3 = (bf16[32,4096]{1,0:T(8,128)(2,1)}, bf16[32,4096]{1,0:T(8,128)(2,1)}, u32[]{:S(2)}, u32[]{:S(2)}) collective-permute-start(bf16[32,4096]{1,0:T(8,128)(2,1)} %get-tuple-element.1028), channel_id=1, source_target_pairs={{0,32},{32,64},{64,96},{96,128},{128,160},{160,192},{192,224},{1,3... | collective-permute-start | bytes 786440 | tf_op jit(solution)/shard_map/while/body/eval_jaxpr/ppermute | solution.py:16
  699.4 26.0 %collective-permute-start.2 = (bf16[32,4096]{1,0:T(8,128)(2,1)}, bf16[32,4096]{1,0:T(8,128)(2,1)}, u32[]{:S(2)}, u32[]{:S(2)}) collective-permute-start(bf16[32,4096]{1,0:T(8,128)(2,1)} %fusion.332), channel_id=1, source_target_pairs={{32,0},{64,32},{96,64},{128,96},{160,128},{192,160},{224,192},{33,... | collective-permute-start | bytes 786440 | tf_op jit(solution)/shard_map/while/body/eval_jaxpr/ppermute | solution.py:16
  700.7 24.8 %collective-permute-start.3 = (bf16[32,4096]{1,0:T(8,128)(2,1)}, bf16[32,4096]{1,0:T(8,128)(2,1)}, u32[]{:S(2)}, u32[]{:S(2)}) collective-permute-start(bf16[32,4096]{1,0:T(8,128)(2,1)} %get-tuple-element.1028), channel_id=1, source_target_pairs={{0,32},{32,64},{64,96},{96,128},{128,160},{160,192},{192,224},{1,3... | collective-permute-start | bytes 786440 | tf_op jit(solution)/shard_map/while/body/eval_jaxpr/ppermute | solution.py:16
  735.9 26.0 %collective-permute-start.2 = (bf16[32,4096]{1,0:T(8,128)(2,1)}, bf16[32,4096]{1,0:T(8,128)(2,1)}, u32[]{:S(2)}, u32[]{:S(2)}) collective-permute-start(bf16[32,4096]{1,0:T(8,128)(2,1)} %fusion.332), channel_id=1, source_target_pairs={{32,0},{64,32},{96,64},{128,96},{160,128},{192,160},{224,192},{33,... | collective-permute-start | bytes 786440 | tf_op jit(solution)/shard_map/while/body/eval_jaxpr/ppermute | solution.py:16
  737.2 24.8 %collective-permute-start.3 = (bf16[32,4096]{1,0:T(8,128)(2,1)}, bf16[32,4096]{1,0:T(8,128)(2,1)}, u32[]{:S(2)}, u32[]{:S(2)}) collective-permute-start(bf16[32,4096]{1,0:T(8,128)(2,1)} %get-tuple-element.1028), channel_id=1, source_target_pairs={{0,32},{32,64},{64,96},{96,128},{128,160},{160,192},{192,224},{1,3... | collective-permute-start | bytes 786440 | tf_op jit(solution)/shard_map/while/body/eval_jaxpr/ppermute | solution.py:16
  763.8 19.6 %collective-permute-start.19 = (bf16[128,4096]{1,0:T(8,128)(2,1)S(1)}, bf16[128,4096]{1,0:T(8,128)(2,1)S(1)}, u32[]{:S(2)}, u32[]{:S(2)}) collective-permute-start(bf16[128,4096]{1,0:T(8,128)(2,1)S(1)} %convert_element_type.624), channel_id=1, source_target_pairs={{0,32},{32,0},{64,96},{96,64},{128,160},{160,128},{192,224},{224,1... | collective-permute-start | bytes 3145736 | tf_op jit(solution)/shard_map/ppermute | solution.py:10
  783.5 31.9 %collective-permute-start.20 = (bf16[128,4096]{1,0:T(8,128)(2,1)S(1)}, bf16[128,4096]{1,0:T(8,128)(2,1)S(1)}, u32[]{:S(2)}, u32[]{:S(2)}) collective-permute-start(bf16[128,4096]{1,0:T(8,128)(2,1)S(1)} %collective-permute-done.19), channel_id=1, source_target_pairs={{0,64},{32,96},{64,0},{96,32},{128,192},{160,224},{192,128},{224,1... | collective-permute-start | bytes 3145736 | tf_op jit(solution)/shard_map/ppermute | solution.py:10
  791.4 32.3 %collective-permute-start.16 = (bf16[4096,128]{1,0:T(8,128)(2,1)S(1)}, bf16[4096,128]{1,0:T(8,128)(2,1)}, u32[]{:S(2)}, u32[]{:S(2)}) collective-permute-start(bf16[4096,128]{1,0:T(8,128)(2,1)S(1)} %convert_element_type.619), channel_id=1, source_target_pairs={{0,32},{32,0},{64,96},{96,64},{128,160},{160,128},{192,224},{224,1... | collective-permute-start | bytes 3145736 | tf_op jit(solution)/shard_map/ppermute | solution.py:10
  815.3 30.6 %collective-permute-start.21 = (bf16[128,4096]{1,0:T(8,128)(2,1)S(1)}, bf16[128,4096]{1,0:T(8,128)(2,1)S(1)}, u32[]{:S(2)}, u32[]{:S(2)}) collective-permute-start(bf16[128,4096]{1,0:T(8,128)(2,1)S(1)} %collective-permute-done.20), channel_id=1, source_target_pairs={{0,128},{32,160},{64,192},{96,224},{128,0},{160,32},{192,64},{224,... | collective-permute-start | bytes 3145736 | tf_op jit(solution)/shard_map/ppermute | solution.py:10
  823.7 36.6 %collective-permute-start.17 = (bf16[4096,128]{1,0:T(8,128)(2,1)}, bf16[4096,128]{1,0:T(8,128)(2,1)}, u32[]{:S(2)}, u32[]{:S(2)}) collective-permute-start(bf16[4096,128]{1,0:T(8,128)(2,1)} %collective-permute-done.16), channel_id=1, source_target_pairs={{0,64},{32,96},{64,0},{96,32},{128,192},{160,224},{192,128},{224,1... | collective-permute-start | bytes 3145736 | tf_op jit(solution)/shard_map/ppermute | solution.py:10
  849.6 226.6 %reduce-scatter.5.cloned.1.call-start = ((), (), s32[]{:S(2)}) async-start(), calls=%async_computation.4 | async-start | bytes 1081344 | tf_op jit(solution)/shard_map/reduce_scatter | solution.py:199
  860.3 16.6 %collective-permute-start.18 = (bf16[4096,128]{1,0:T(8,128)(2,1)}, bf16[4096,128]{1,0:T(8,128)(2,1)S(1)}, u32[]{:S(2)}, u32[]{:S(2)}) collective-permute-start(bf16[4096,128]{1,0:T(8,128)(2,1)} %collective-permute-done.17), channel_id=1, source_target_pairs={{0,128},{32,160},{64,192},{96,224},{128,0},{160,32},{192,64},{224,... | collective-permute-start | bytes 3145736 | tf_op jit(solution)/shard_map/ppermute | solution.py:10
  (86 other events, 406.8 us)
Sparse Core Ops, SparseCore 0:
  23.8 66.0 all-gather.2
  92.4 63.5 all-gather.4
  849.7 110.3 reduce-scatter.6
  962.5 113.7 reduce-scatter.4
where the time goes:
time: 1100 us; the launch traced here: 1080 us
  waiting for transfers between devices  354 us (32%)
  matrix products  304 us (28%)
  starting transfers between devices  206 us (19%)
  other arithmetic  107 us (10%)
  blocking collectives  80.1 us (7%)
  local copies, waits for them, and re-layouts  15.7 us (1%)
  between operations  14.6 us (1%)
    ppermute x36, starting transfers between devices, passed_along(): lax.ppermute(value, axis, [(source, source + steps) for source in range(i...  152 us
    dot_general x54, matrix products, apply_layer(): jnp.dot(reduced, second_weight, preferred_element_type=jnp.float32)  122 us
    reduce_scatter x1, waiting for transfers between devices, per_device(): lax.psum_scatter(pair_sums[1].astype(jnp.bfloat16), 'dp', scatter_dimensi...  115 us
    ppermute x18, waiting for transfers between devices, partner(): lax.ppermute(shard, axis, [(i, i ^ 1 << distance) for i in range(lax.axis...  110 us
    dot_general x72, matrix products, apply_layer(): jnp.einsum('hqk,khd->qhd', probabilities, split_heads, preferred_element_...  77 us
    dot_general x36, matrix products, apply_layer(): jnp.dot(mixed_heads, first_weight, preferred_element_type=jnp.float32)  69.7 us
    all_gather x1, waiting for transfers between devices, per_device(): lax.all_gather(stacked[1], 'dp', axis=1, tiled=True)  66.1 us
    ppermute x18, starting transfers between devices, partner(): lax.ppermute(shard, axis, [(i, i ^ 1 << distance) for i in range(lax.axis...  53.8 us
  transfers between devices with their start and end apart: 58, of which 30 were waited for; matrix products, arithmetic and copies ran while one was open for 21% of the time, Pallas kernels for 0%

commit v1 on v0

v1 whole, which is shorter than its diff:
```python
import jax
import jax.numpy as jnp
from jax import lax
from jax.experimental import pallas as pl
from jax.experimental.pallas import tpu as pltpu
from jax.sharding import PartitionSpec as P

MESH = pl.DeviceIdType.MESH
F32 = jnp.float32
BF16 = jnp.bfloat16
L = 8
NX = 4
NZ = 8
NY = 4
HD = 128
T = 64
C = 1024
PR = 144
D = 4096


def dot(a, b):
    return lax.dot_general(a, b, (((1,), (0,)), ((), ())), preferred_element_type=F32)


def dot_nt(a, b):
    return lax.dot_general(a, b, (((1,), (1,)), ((), ())), preferred_element_type=F32)


def pair_blocks(v):
    zero = jnp.zeros((T, HD), v.dtype)
    top = jnp.concatenate((v[:, :HD], zero), axis=1)
    low = jnp.concatenate((zero, v[:, HD:]), axis=1)
    return jnp.concatenate((top, low), axis=0)


def token_rows(p):
    both = jnp.concatenate((p, p), axis=0)
    high = both.astype(BF16)
    low = (both - high.astype(F32)).astype(BF16)
    return dot_nt(jnp.ones((16, 2 * HD), BF16), jnp.concatenate((high, low), axis=1))[:8]


def to_column(row):
    return jnp.transpose(jnp.broadcast_to(row[0:1], (HD, HD)))[:T]


def twice(v):
    return jnp.concatenate((v, v), axis=1)


def kernel(
    tok, cot, starts, counts, gain_in, first_in, second_in,
    gain_out, first_out, second_out,
    chunk, wbuf, X, H, M, ES, Fr, R, RR, SS, BB, AA, PS, PT, DYP, MK, MKT,
    G, RA, SA, RB, SB, RC,
    in_sem, s1_send, s1_recv, z_send, z_recv, k_send, k_recv, tp_send, tp_recv,
    a_send, a_recv, b_send, b_recv, c_send, c_recv,
):
    p = lax.axis_index("pipe")
    d = lax.axis_index("dp")
    x, yh = p // 2, p % 2
    yl, z, c = d // 16, (d // 2) % 8, d % 2
    y = 2 * yh + yl
    k_own = z % 4

    def x_peer(i):
        return (((x + i) % NX) * 2 + yh, d)

    def z_peer(zz):
        return (p, yl * 16 + zz * 2 + c)

    core_peer = (p, d + 1 - 2 * c)

    def holder(q):
        yy, h = q // 2, q % 2
        return ((d // 8) * 2 + yy // 2, (yy % 2) * 16 + (2 * k_own + h) * 2 + c)

    def owner(l):
        return (l, 8 * x + 2 * (z // 2) + c)

    def is_me(dev):
        return (dev[0] == p) & (dev[1] == d)

    def remote(src, dst, ss, rs, dev):
        return pltpu.make_async_remote_copy(
            src_ref=src, dst_ref=dst, send_sem=ss, recv_sem=rs, device_id=dev, device_id_type=MESH
        )

    cols = pl.ds(pl.multiple_of(x * C, C), C)
    loads = []
    for b in range(2):
        rows = pl.ds(32 * b, 32)
        loads.append(pltpu.make_async_copy(tok.at[yh, b, :, cols], X.at[0, rows, :], in_sem.at[b]))
        loads.append(pltpu.make_async_copy(cot.at[yh, b, :, cols], M.at[L, rows, :], in_sem.at[2 + b]))
    for load in loads:
        load.start()

    barrier = pltpu.get_barrier_semaphore()

    def greet(dev):
        pl.semaphore_signal(barrier, inc=1, device_id=dev, device_id_type=MESH)

    greet(core_peer)

    def greet_x(i, carry):
        greet(x_peer(i))
        return carry

    def greet_z(i, carry):
        greet(z_peer((z + i) % NZ))
        return carry

    def greet_far(q, carry):
        for dev in (holder(q), owner(q)):
            @pl.when(jnp.logical_not(is_me(dev)))
            def _():
                greet(dev)
        return carry

    lax.fori_loop(1, NX, greet_x, 0)
    lax.fori_loop(1, NZ, greet_z, 0)
    lax.fori_loop(0, 8, greet_far, 0)

    for h in range(2):
        chunk[h, 0:64, :] = first_in[0, 64 * h : 64 * h + 64, :]
        chunk[h, 64:128, :] = second_in[0, 64 * h : 64 * h + 64, :]
        chunk[h, 128:144, :] = jnp.broadcast_to(gain_in[0:1, :].astype(F32), (16, HD)).astype(BF16)

    row_id = lax.broadcasted_iota(jnp.int32, (T, HD), 0)
    lane_id = lax.broadcasted_iota(jnp.int32, (T, HD), 1) % T

    def documents(index):
        second_mb = index >= 32
        pos = jnp.where(second_mb, index - 32, index)
        doc = jnp.zeros((T, HD), jnp.int32)
        count = jnp.where(second_mb, counts[yh, 1], counts[yh, 0])
        for j in range(4):
            start = jnp.where(second_mb, starts[yh, 1, j], starts[yh, 0, j])
            doc = doc + jnp.where((start <= pos) & (j < count), 1, 0)
        return doc + jnp.where(second_mb, 64, 0)

    same = documents(row_id) == documents(lane_id)
    MK[...] = jnp.where(same & (lane_id <= row_id), 1.0, 0.0)
    MKT[...] = jnp.where(same & (row_id <= lane_id), 1.0, 0.0)
    Fr[L] = jnp.zeros((8, HD), F32)
    for i in range(NX):
        BB[L, i] = jnp.zeros((T, HD), BF16)
    half_r = lax.broadcasted_iota(jnp.int32, (HD, HD), 0) // T
    half_l = lax.broadcasted_iota(jnp.int32, (HD, HD), 1) // T
    ones_blocks = jnp.where(half_r == half_l, 1.0, 0.0).astype(BF16)

    me_holder = jnp.int32(0)
    me_owner = jnp.int32(0)
    for q in range(8):
        me_holder = me_holder + jnp.where(is_me(holder(q)), 1, 0)
        me_owner = me_owner + jnp.where(is_me(owner(q)), 1, 0)
    pl.semaphore_wait(barrier, 27 - me_holder - me_owner)

    def s1_copy(q):
        h = q % 2
        return remote(
            chunk.at[h], wbuf.at[p, c, 2 * k_own + h], s1_send.at[q], s1_recv.at[p], holder(q)
        )

    def s1_start(q, carry):
        mine = is_me(holder(q))
        h = q % 2

        @pl.when(mine)
        def _():
            pltpu.make_async_copy(
                chunk.at[h], wbuf.at[p, c, 2 * k_own + h], s1_recv.at[p]
            ).start()

        @pl.when(jnp.logical_not(mine))
        def _():
            s1_copy(q).start()

        return carry

    lax.fori_loop(0, 8, s1_start, 0)

    def tp_copy(kind, buf, e, i):
        slot = buf.at[e, x]
        return remote(slot, slot, tp_send.at[kind, e, i], tp_recv.at[kind, e, x], x_peer(i))

    def tp_send_all(kind, buf, e):
        for i in (2, 1, 3):
            tp_copy(kind, buf, e, i).start()

    def tp_wait(kind, buf, e):
        for i in (1, 3, 2):
            src = (x + i) % NX
            slot = buf.at[e, src]
            remote(slot, slot, tp_send.at[kind, e, i], tp_recv.at[kind, e, src], x_peer(i)).wait_recv()

    def tp_sum(buf, e):
        total = buf[e, 0].astype(F32)
        for i in range(1, NX):
            total = total + buf[e, i].astype(F32)
        return total

    def send_squares(e, value):
        acc = jnp.zeros((T, HD), F32)
        for j in range(C // HD):
            piece = value[:, HD * j : HD * j + HD]
            acc = acc + piece * piece
        SS[e, x] = token_rows(acc)
        tp_send_all(1, SS, e)

    loads[0].wait()
    loads[2].wait()
    send_squares(0, X[0].astype(F32))

    def z_copy(l, i):
        slot = wbuf.at[l, c, z]
        return remote(slot, slot, z_send.at[l, i], z_recv.at[l, z], z_peer((z + i) % NZ))

    def spread(l, carry):
        slot = wbuf.at[l, c, z]
        remote(slot, slot, s1_send.at[0], s1_recv.at[l], core_peer).wait_recv()

        def go(i, inner):
            z_copy(l, i).start()
            return inner

        return lax.fori_loop(1, NZ, go, carry)

    lax.fori_loop(0, L, spread, 0)

    def k_copy(l, which):
        slot = wbuf.at[l, which]
        return remote(slot, slot, k_send.at[l], k_recv.at[l], core_peer)

    def to_core(l):
        def one(i, inner):
            src = (z + i) % NZ
            slot = wbuf.at[l, c, src]
            remote(slot, slot, z_send.at[l, i], z_recv.at[l, src], z_peer(src)).wait_recv()
            return inner

        lax.fori_loop(1, NZ, one, 0)
        k_copy(l, c).start()

    to_core(0)
    to_core(1)

    def w1(l, t):
        return jnp.concatenate(
            [wbuf[l, cc, 2 * t + h, 0:64, :] for cc in range(2) for h in range(2)], axis=0
        )

    def w2(l, t):
        heads = [
            jnp.concatenate([wbuf[l, cc, 2 * t + h, 64:128, :] for h in range(2)], axis=0)
            for cc in range(2)
        ]
        return jnp.concatenate(heads, axis=1)

    def gains(l, t):
        heads = []
        for cc in range(2):
            g16 = wbuf[l, cc, 2 * t, 128:144, :].astype(F32)
            heads.append(jnp.concatenate([g16] * 4, axis=0))
        return jnp.concatenate(heads, axis=1)

    def cols_of(t):
        return slice(256 * t, 256 * t + 256)

    def lanes_of(t):
        return slice(HD * t, HD * t + HD)

    def forward(l, carry):
        k_copy(l, 1 - c).wait_recv()
        raw = []
        for t in range(4):
            h = (X[l, :, cols_of(t)].astype(F32) * gains(l, t)).astype(BF16)
            H[l, :, cols_of(t)] = h
            raw.append(dot_nt(h, pair_blocks(h)))
        tp_wait(1, SS, l)
        f_row = lax.rsqrt(tp_sum(SS, l) * (1.0 / D) + 1e-05)
        Fr[l] = f_row
        f_key = f_row[0:1]
        scale = to_column(f_row) * f_key * (1.0 / HD)
        mask = MK[...]
        part = jnp.zeros((T, HD), F32)
        for t in range(4):
            e = jnp.exp(raw[t] * scale).astype(BF16)
            ES[l, :, lanes_of(t)] = e
            e = (e.astype(F32) * mask).astype(BF16)
            sums = dot(e, ones_blocks)
            prob = (e.astype(F32) * f_key / sums).astype(BF16)
            mixed = dot(prob, pair_blocks(H[l, :, cols_of(t)])).astype(BF16)
            M[l, :, cols_of(t)] = mixed
            part = part + dot(mixed, w1(l, t))
        RR[l, x] = part.astype(BF16)
        tp_send_all(0, RR, l)

        @pl.when(l > 0)
        def _():
            cross = jnp.zeros((T, HD), F32)
            for t in range(4):
                cross = cross + dot_nt(X[l, :, cols_of(t)], w2(l - 1, t))
            BB[l, x] = cross.astype(BF16)
            tp_send_all(2, BB, l)

        @pl.when(l == L - 1)
        def _():
            loads[1].wait()
            loads[3].wait()
            acc = jnp.zeros((T, HD), F32)
            for t in range(4):
                acc = acc + dot_nt(M[L, :, cols_of(t)], w2(L - 1, t))
            AA[L - 1, x, 0:64, :] = acc.astype(BF16)
            AA[L - 1, x, 64:80, :] = jnp.zeros((16, HD), BF16)
            tp_send_all(3, AA, L - 1)
            DYP[...] = M[L].astype(F32)

        @pl.when(l + 2 < L)
        def _():
            to_core(l + 2)

        tp_wait(0, RR, l)
        r = tp_sum(RR, l).astype(BF16)
        R[l] = r
        for t in range(4):
            X[l + 1, :, cols_of(t)] = (
                X[l, :, cols_of(t)].astype(F32) + dot(r, w2(l, t))
            ).astype(BF16)

        @pl.when(l < L - 1)
        def _():
            send_squares(l + 1, X[l + 1].astype(F32))

        return carry

    lax.fori_loop(0, L, forward, 0)

    def a_copy(l, which):
        return remote(G.at[l, which], RA.at[l], a_send.at[l], a_recv.at[l], core_peer)

    def b_copy(l, i):
        zz = (z + i) % NZ
        return remote(SA.at[l, zz], RB.at[l, z], b_send.at[l, i], b_recv.at[l, z], z_peer(zz))

    def c_copy(l):
        return remote(SB.at[l], RC.at[y, z % 2], c_send.at[l], c_recv.at[y, z % 2], owner(l))

    def one_layer(l):
        f_row = Fr[l]
        f_key = f_row[0:1]
        f_col = to_column(f_row)
        mask = MK[...]
        mask_t = MKT[...]
        for t in range(4):
            es = ES[l, :, lanes_of(t)].astype(F32)
            e = es * mask
            sums = dot(e.astype(BF16), ones_blocks)
            PS[:, lanes_of(t)] = e / sums
            et = es * mask_t
            PT[:, lanes_of(t)] = et / jnp.sum(et, axis=0, keepdims=True)

        @pl.when(l < L - 1)
        def _():
            tp_wait(2, BB, l + 1)

        tp_wait(3, AA, l)
        total = tp_sum(AA, l)
        s_row = total[64:72] + total[72:80]
        f_next = Fr[l + 1]
        coef = to_column(f_next * f_next * f_next * s_row * (1.0 / D))
        dr = total[:64] - coef * tp_sum(BB, l + 1)
        dr_b = dr.astype(BF16)
        coef2 = twice(coef)
        f_col2 = twice(f_col)
        s_part = jnp.zeros((T, HD), F32)
        acc = jnp.zeros((T, HD), F32)
        below = jnp.maximum(l - 1, 0)
        for t in range(4):
            h = H[l, :, cols_of(t)]
            blocks = pair_blocks(h)
            dm = dot_nt(dr_b, w1(l, t)).astype(BF16)
            dm_blocks = pair_blocks(dm)
            prob = PS[:, lanes_of(t)]
            prob_t = PT[:, lanes_of(t)]
            dp = dot_nt(dm, blocks) * f_key
            dp_t = dot_nt(h, dm_blocks) * f_col
            inner = dot((prob * dp).astype(BF16), ones_blocks)
            ds = prob * (dp - inner)
            inner_t = jnp.sum(prob_t * dp_t, axis=0, keepdims=True)
            ds_t = prob_t * (dp_t - inner_t)
            both = (ds + ds_t) * f_key * (1.0 / HD)
            left = jnp.concatenate((both.astype(BF16), prob_t.astype(BF16)), axis=1)
            dn = dot(left, jnp.concatenate((blocks, dm_blocks), axis=0))
            xs = X[l, :, cols_of(t)].astype(F32)
            gdn = dn * gains(l, t)
            dy = DYP[:, cols_of(t)] - X[l + 1, :, cols_of(t)].astype(F32) * coef2
            M[L, :, cols_of(t)] = dy.astype(BF16)
            dyp = dy + gdn * f_col2
            DYP[:, cols_of(t)] = dyp
            acc = acc + dot_nt(dyp.astype(BF16), w2(below, t))
            prod = gdn * xs
            s_part = s_part + prod[:, :HD] + prod[:, HD:]
            dgain = jnp.sum(dn * xs * f_col2, axis=0, keepdims=True)
            wide = jnp.broadcast_to(dgain, (16, 256)).astype(BF16)
            for cc in range(2):
                for h2 in range(2):
                    G[l, cc, 2 * t + h2, 128:144, :] = wide[:, HD * cc : HD * cc + HD]

        @pl.when(l > 0)
        def _():
            s_new = token_rows(s_part)
            s_high = s_new.astype(BF16).astype(F32)
            AA[below, x, 0:64, :] = acc.astype(BF16)
            AA[below, x, 64:80, :] = jnp.concatenate((s_high, s_new - s_high), axis=0).astype(BF16)
            tp_send_all(3, AA, below)

        zeros = jnp.zeros((T, HD), F32)
        dr_t = jnp.transpose(jnp.concatenate((dr, zeros), axis=0)).astype(BF16)[:, :T]
        r_t = jnp.transpose(jnp.concatenate((R[l].astype(F32), zeros), axis=0)).astype(BF16)[:, :T]
        for t in range(4):
            g1 = dot(dr_t, M[l, :, cols_of(t)]).astype(BF16)
            g2 = dot(r_t, M[L, :, cols_of(t)]).astype(BF16)
            for cc in range(2):
                for h2 in range(2):
                    rows = slice(64 * h2, 64 * h2 + 64)
                    lanes = slice(HD * cc, HD * cc + HD)
                    G[l, cc, 2 * t + h2, 0:64, :] = g1[rows, lanes]
                    G[l, cc, 2 * t + h2, 64:128, :] = g2[rows, lanes]
        a_copy(l, 1 - c).start()

    def core_sums(l):
        a_copy(l, 1 - c).wait_recv()

        def one(i, carry):
            SA[l, i] = (G[l, c, i].astype(F32) + RA[l, i].astype(F32)).astype(BF16)
            return carry

        lax.fori_loop(0, NZ, one, 0)
        RB[l, z] = SA[l, z]

        def go(i, carry):
            b_copy(l, i).start()
            return carry

        lax.fori_loop(1, NZ, go, 0)

    def z_sums(l):
        def one(i, carry):
            src = (z + i) % NZ
            remote(
                SA.at[l, src], RB.at[l, src], b_send.at[l, i], b_recv.at[l, src], z_peer(src)
            ).wait_recv()
            return carry

        lax.fori_loop(1, NZ, one, 0)
        total = RB[l, 0].astype(F32)
        for i in range(1, NZ):
            total = total + RB[l, i].astype(F32)
        SB[l] = total.astype(BF16)
        mine = is_me(owner(l))

        @pl.when(mine)
        def _():
            pltpu.make_async_copy(SB.at[l], RC.at[y, z % 2], c_recv.at[y, z % 2]).start()

        @pl.when(jnp.logical_not(mine))
        def _():
            c_copy(l).start()

    def backward(i, carry):
        @pl.when(i < L)
        def _():
            one_layer(L - 1 - i)

        @pl.when((i >= 1) & (i < L + 1))
        def _():
            core_sums(L - i)

        @pl.when(i >= 2)
        def _():
            z_sums(L + 1 - i)

        return carry

    lax.fori_loop(0, L + 2, backward, 0)

    for yy in range(NY):
        for h in range(2):
            remote(
                SB.at[0], RC.at[yy, h], c_send.at[0], c_recv.at[yy, h], core_peer
            ).wait_recv()
    halves = []
    for h in range(2):
        total = RC[0, h].astype(F32)
        for yy in range(1, NY):
            total = total + RC[yy, h].astype(F32)
        halves.append(total)
    first_out[0] = jnp.transpose(jnp.concatenate((halves[0][0:64], halves[1][0:64]), axis=0))
    second_out[0] = jnp.concatenate((halves[0][64:128], halves[1][64:128]), axis=0)
    gain_out[...] = halves[0][128:129]

    def drain_far(q, carry):
        @pl.when(jnp.logical_not(is_me(holder(q))))
        def _():
            s1_copy(q).wait_send()

        @pl.when(jnp.logical_not(is_me(owner(q))))
        def _():
            c_copy(q).wait_send()

        return carry

    lax.fori_loop(0, 8, drain_far, 0)

    def drain(l, carry):
        k_copy(l, c).wait_send()
        a_copy(l, 1 - c).wait_send()
        for i in range(1, NX):
            tp_copy(0, RR, l, i).wait_send()
            tp_copy(1, SS, l, i).wait_send()
            tp_copy(3, AA, l, i).wait_send()

            @pl.when(l > 0)
            def _():
                tp_copy(2, BB, l, i).wait_send()

        def one(i, inner):
            z_copy(l, i).wait_send()
            b_copy(l, i).wait_send()
            return inner

        return lax.fori_loop(1, NZ, one, carry)

    lax.fori_loop(0, L, drain, 0)


def per_device(tokens, cotangents, starts, counts, layer_gains, first_map, second_map):
    vmem = pl.BlockSpec(memory_space=pltpu.VMEM)
    smem = pl.BlockSpec(memory_space=pltpu.SMEM)
    hbm = pl.BlockSpec(memory_space=pl.ANY)
    sem = pltpu.SemaphoreType.DMA
    return pl.pallas_call(
        kernel,
        out_shape=(
            jax.ShapeDtypeStruct((1, HD), F32),
            jax.ShapeDtypeStruct((1, HD, HD), F32),
            jax.ShapeDtypeStruct((1, HD, HD), F32),
        ),
        in_specs=[hbm, hbm, smem, smem, vmem, vmem, vmem],
        out_specs=(vmem, vmem, vmem),
        scratch_shapes=[
            pltpu.VMEM((2, PR, HD), BF16),
            pltpu.VMEM((L, 2, NZ, PR, HD), BF16),
            pltpu.VMEM((L + 1, T, C), BF16),
            pltpu.VMEM((L, T, C), BF16),
            pltpu.VMEM((L + 1, T, C), BF16),
            pltpu.VMEM((L, T, 4 * HD), BF16),
            pltpu.VMEM((L + 1, 8, HD), F32),
            pltpu.VMEM((L, T, HD), BF16),
            pltpu.VMEM((L, NX, T, HD), BF16),
            pltpu.VMEM((L, NX, 8, HD), F32),
            pltpu.VMEM((L + 1, NX, T, HD), BF16),
            pltpu.VMEM((L, NX, 80, HD), BF16),
            pltpu.VMEM((T, 4 * HD), F32),
            pltpu.VMEM((T, 4 * HD), F32),
            pltpu.VMEM((T, C), F32),
            pltpu.VMEM((T, HD), F32),
            pltpu.VMEM((T, HD), F32),
            pltpu.VMEM((L, 2, NZ, PR, HD), BF16),
            pltpu.VMEM((L, NZ, PR, HD), BF16),
            pltpu.VMEM((L, NZ, PR, HD), BF16),
            pltpu.VMEM((L, NZ, PR, HD), BF16),
            pltpu.VMEM((L, PR, HD), BF16),
            pltpu.VMEM((NY, 2, PR, HD), BF16),
            sem((4,)),
            sem((8,)), sem((L,)),
            sem((L, NZ)), sem((L, NZ)),
            sem((L,)), sem((L,)),
            sem((4, L, NX)), sem((4, L, NX)),
            sem((L,)), sem((L,)),
            sem((L, NZ)), sem((L, NZ)),
            sem((L,)), sem((NY, 2)),
        ],
        compiler_params=pltpu.CompilerParams(
            collective_id=0, has_side_effects=True, vmem_limit_bytes=48 * 1024 * 1024
        ),
    )(tokens, cotangents, starts, counts, layer_gains, first_map, second_map)


def solution(mesh):
    in_specs = (
        P(None, "dp", None, None),
        P(None, "dp", None, None),
        P(None, "dp", None),
        P(None, "dp"),
        P("pipe", "dp"),
        P("pipe", "dp", None),
        P("pipe", None, "dp"),
    )
    out_specs = (P("pipe", "dp"), P("pipe", "dp", None), P("pipe", None, "dp"))
    return jax.shard_map(
        per_device, mesh=mesh, in_specs=in_specs, out_specs=out_specs, check_vma=False
    )
```

time: 1100 us -> 212 us (0.19); the launches traced: 1080 us -> 208 us
  waiting for transfers between devices: 354 us -> 0 us
  matrix products: 304 us -> 0 us
  starting transfers between devices: 206 us -> 0 us
  Pallas kernels: 0 us -> 200 us
  other arithmetic: 107 us -> 0 us
  blocking collectives: 80.1 us -> 0 us
  between operations: 14.6 us -> 0.66 us
    dot_general x234 -> x0, matrix products: 304 us -> none  [the longest x54 122 us: apply_layer(): jnp.dot(reduced, second_weight, preferred_element_type=jnp.float32)]
    ppermute x54 -> x0, starting transfers between devices: 205 us -> none  [the longest x36 152 us: passed_along(): lax.ppermute(value, axis, [(source, source + steps) for source in range(i...]
    pallas_call x0 -> x1, Pallas kernels: none -> 200 us  [per_device(): pl.pallas_call(kernel, out_shape=(jax.ShapeDtypeStruct((1, HD), F32), jax...]
    ppermute x54 -> x0, waiting for transfers between devices: 151 us -> none  [the longest x18 110 us: partner(): lax.ppermute(shard, axis, [(i, i ^ 1 << distance) for i in range(lax.axis...]
    reduce_scatter x1 -> x0, waiting for transfers between devices: 115 us -> none  [per_device(): lax.psum_scatter(pair_sums[1].astype(jnp.bfloat16), 'dp', scatter_dimensi...]
    all_gather x2 -> x0, waiting for transfers between devices: 67.7 us -> none  [the longest x1 66.1 us: per_device(): lax.all_gather(stacked[1], 'dp', axis=1, tiled=True)]
    unnamed x1 -> x0, blocking collectives: 46.6 us -> none
    all_gather x1 -> x0, blocking collectives: 33.5 us -> none  [per_device(): lax.all_gather(stacked[0], 'dp', axis=1, tiled=True)]
  transfers between devices with their start and end apart: 58 -> 0, of which waited for: 30 -> 0; matrix products, arithmetic and copies ran while one was open for 21% -> 0% of each run, Pallas kernels for 0% -> 0%
where the time goes in v1:
time: 212 us; the launch traced here: 208 us
  Pallas kernels  200 us (94%)
  local copies, waits for them, and re-layouts  7.74 us (4%)
    pallas_call x1, Pallas kernels, per_device(): pl.pallas_call(kernel, out_shape=(jax.ShapeDtypeStruct((1, HD), F32), jax...  200 us
    unnamed x17, local copies, waits for them, and re-layouts  7.74 us

profile of v1, /device:TPU:64, one launch (start us, length us, event | category | flops | bytes accessed | tf_op | source)
XLA Modules:
  0.0 208.1 jit_solution(13475101557282040185)
XLA Ops:
  0.6 0.0 copy-start
  0.6 1.2 copy-done
  1.9 0.0 copy-start.1
  1.9 1.2 copy-done.1
  3.1 0.0 copy-start.2
  3.1 0.8 copy-done.2
  3.8 0.0 copy-start.3
  3.8 0.8 copy-done.3
  4.6 0.0 copy-start.4
  4.6 0.7 copy-done.4
  5.3 0.0 copy-start.5
  5.3 0.7 copy-done.5
  6.0 0.0 copy-start.6
  6.0 0.7 copy-done.6
  6.6 199.7 %shard_map.94 = (f32[1,128]{1,0:T(1,128)S(1)}, f32[1,128,128]{2,1,0:T(8,128)S(1)}, f32[1,128,128]{2,1,0:T(8,128)S(1)}) custom-call(bf16[2,2,32,4096]{3,2,1,0:T(8,128)(2,1)S(1)} %copy-done, bf16[2,2,32,4096]{3,2,1,0:T(8,128)(2,1)S(1)} %copy-done.1, s32[2,2,4]{2,1,0:T(2,128)S(1)} %copy-done.4, s32[2,2]{1,0:T(2,128)S(1)} %copy-done.5, ...), custom_call_target="tpu_custom_call" | custom-call | tf_op jit(solution)/shard_map/pallas_call | solution.py:544
  206.3 0.5 copy.13
  206.9 0.6 copy.14
  207.5 0.6 copy.15
Async XLA Ops:
  0.6 1.2 copy-start
  1.9 1.2 copy-start.1
  3.1 0.8 copy-start.2
  3.8 0.8 copy-start.3
  4.6 0.7 copy-start.4
  5.3 0.7 copy-start.5
  6.0 0.7 copy-start.6

commit v2 on v1

v2 whole, which is shorter than its diff:
```python
import jax
import jax.numpy as jnp
from jax import lax
from jax.experimental import pallas as pl
from jax.experimental.pallas import tpu as pltpu
from jax.sharding import PartitionSpec as P

MESH = pl.DeviceIdType.MESH
F32 = jnp.float32
BF16 = jnp.bfloat16
L = 8
NX = 4
NZ = 8
NY = 4
HD = 128
T = 64
C = 1024
PR = 40
D = 4096
VMEM_LIMIT = 67043328 - 136 * 1024


def dot(a, b):
    return lax.dot_general(a, b, (((1,), (0,)), ((), ())), preferred_element_type=F32)


def dot_nt(a, b):
    return lax.dot_general(a, b, (((1,), (1,)), ((), ())), preferred_element_type=F32)


def pair_blocks(v):
    zero = jnp.zeros((T, HD), v.dtype)
    top = jnp.concatenate((v[:, :HD], zero), axis=1)
    low = jnp.concatenate((zero, v[:, HD:]), axis=1)
    return jnp.concatenate((top, low), axis=0)


def token_rows(p):
    both = jnp.concatenate((p, p), axis=0)
    high = both.astype(BF16)
    low = (both - high.astype(F32)).astype(BF16)
    return dot_nt(jnp.ones((16, 2 * HD), BF16), jnp.concatenate((high, low), axis=1))[:8]


def to_column(row):
    return jnp.transpose(jnp.broadcast_to(row[0:1], (HD, HD)))[:T]


def twice(v):
    return jnp.concatenate((v, v), axis=1)


def kernel(
    tok, cot, starts, counts, gain_in, first_in, second_in,
    gain_out, first_out, second_out,
    chunk, own_gain, own_first, own_second, wbuf, X, H, M, ES, Fr, R, RR, SS, BB, AA,
    PS, PT, DYP, MK, MKT, G, RA, SA, RB, SB, RC, SD, RD,
    in_sem, sent, s1_recv, z_recv, y_recv, k_recv, tp_recv, b_recv,
    ga_recv, gy_recv, gz_recv, go_recv,
):
    p = lax.axis_index("pipe")
    d = lax.axis_index("dp")
    x, yh = p // 2, p % 2
    yl, z, c = d // 16, (d // 2) % 8, d % 2
    y = 2 * yh + yl
    k_own = z % 4

    def x_peer(i):
        return (((x + i) % NX) * 2 + yh, d)

    def z_peer(zz):
        return (p, yl * 16 + zz * 2 + c)

    def y_peer(yy):
        return (x * 2 + yy // 2, (yy % 2) * 16 + z * 2 + c)

    core_peer = (p, d + 1 - 2 * c)

    def holder(q):
        yy, h = q // 2, q % 2
        return ((d // 8) * 2 + yy // 2, (yy % 2) * 16 + (2 * k_own + h) * 2 + c)

    def owner(l):
        return (l, 8 * x + 2 * (z // 2) + c)

    def is_me(dev):
        return (dev[0] == p) & (dev[1] == d)

    def arrived(ref, sem):
        pltpu.make_async_copy(ref, ref, sem).wait()

    def remote(src, dst, ss, rs, dev):
        return pltpu.make_async_remote_copy(
            src_ref=src, dst_ref=dst, send_sem=ss, recv_sem=rs, device_id=dev, device_id_type=MESH
        )

    cols = pl.ds(pl.multiple_of(x * C, C), C)
    loads = []
    for b in range(2):
        rows = pl.ds(32 * b, 32)
        loads.append(pltpu.make_async_copy(tok.at[yh, b, :, cols], X.at[0, rows, :], in_sem.at[b]))
        loads.append(pltpu.make_async_copy(cot.at[yh, b, :, cols], M.at[L, rows, :], in_sem.at[2 + b]))
    chunk_loads = [
        pltpu.make_async_copy(first_in, own_first, in_sem.at[4]),
        pltpu.make_async_copy(second_in, own_second, in_sem.at[5]),
        pltpu.make_async_copy(gain_in, own_gain, in_sem.at[6]),
    ]
    for load in chunk_loads + loads:
        load.start()

    barrier = pltpu.get_barrier_semaphore()

    def greet(dev):
        pl.semaphore_signal(barrier, inc=1, device_id=dev, device_id_type=MESH)

    def greet_x(i, carry):
        greet(x_peer(i))
        return carry

    def greet_z(i, carry):
        greet(z_peer((z + i) % NZ))
        return carry

    def greet_y(i, carry):
        greet(y_peer((y + i) % NY))
        return carry

    def greet_far(q, carry):
        for dev in (holder(q), owner(q)):
            @pl.when(jnp.logical_not(is_me(dev)))
            def _():
                greet(dev)
        return carry

    lax.fori_loop(0, 8, greet_far, 0)
    lax.fori_loop(1, NZ, greet_z, 0)
    lax.fori_loop(1, NY, greet_y, 0)
    lax.fori_loop(1, NX, greet_x, 0)
    greet(core_peer)

    row_id = lax.broadcasted_iota(jnp.int32, (T, HD), 0)
    lane_id = lax.broadcasted_iota(jnp.int32, (T, HD), 1) % T

    def documents(index):
        second_mb = index >= 32
        pos = jnp.where(second_mb, index - 32, index)
        doc = jnp.zeros((T, HD), jnp.int32)
        count = jnp.where(second_mb, counts[yh, 1], counts[yh, 0])
        for j in range(4):
            start = jnp.where(second_mb, starts[yh, 1, j], starts[yh, 0, j])
            doc = doc + jnp.where((start <= pos) & (j < count), 1, 0)
        return doc + jnp.where(second_mb, 64, 0)

    same = documents(row_id) == documents(lane_id)
    MK[...] = jnp.where(same & (lane_id <= row_id), 1.0, 0.0)
    MKT[...] = jnp.where(same & (row_id <= lane_id), 1.0, 0.0)
    Fr[L] = jnp.zeros((8, HD), F32)
    for i in range(NX):
        BB[L, i] = jnp.zeros((T, HD), BF16)
    half_r = lax.broadcasted_iota(jnp.int32, (HD, HD), 0) // T
    half_l = lax.broadcasted_iota(jnp.int32, (HD, HD), 1) // T
    ones_blocks = jnp.where(half_r == half_l, 1.0, 0.0).astype(BF16)

    me_holder = jnp.int32(0)
    me_owner = jnp.int32(0)
    for q in range(8):
        me_holder = me_holder + jnp.where(is_me(holder(q)), 1, 0)
        me_owner = me_owner + jnp.where(is_me(owner(q)), 1, 0)
    for load in chunk_loads:
        load.wait()
    for q in range(8):
        rows = slice(64 * (q % 2) + 16 * (q // 2), 64 * (q % 2) + 16 * (q // 2) + 16)
        chunk[q, 0:16, :] = own_first[0, rows, :]
        chunk[q, 16:32, :] = own_second[0, rows, :]
        chunk[q, 32:40, :] = jnp.broadcast_to(own_gain[0:1, :].astype(F32), (8, HD)).astype(BF16)
    pl.semaphore_wait(barrier, 30 - me_holder - me_owner)

    def s1_start(q, carry):
        mine = is_me(holder(q))
        slot = wbuf.at[p, c, q // 2, 2 * k_own + q % 2]

        @pl.when(mine)
        def _():
            pltpu.make_async_copy(chunk.at[q], slot, s1_recv.at[p]).start()

        @pl.when(jnp.logical_not(mine))
        def _():
            remote(chunk.at[q], slot, sent.at[0], s1_recv.at[p], holder(q)).start()

        return carry

    lax.fori_loop(0, 8, s1_start, 0)

    def tp_send_all(kind, buf, e, sem):
        slot = buf.at[e, x]
        for i in (2, 1, 3):
            remote(slot, slot, sent.at[kind], sem, x_peer(i)).start()

    def tp_wait(buf, e, sem):
        arrived(buf.at[e, 0 : NX - 1], sem)

    def tp_sum(buf, e):
        total = buf[e, 0].astype(F32)
        for i in range(1, NX):
            total = total + buf[e, i].astype(F32)
        return total

    def send_squares(e, value):
        acc = jnp.zeros((T, HD), F32)
        for j in range(C // HD):
            piece = value[:, HD * j : HD * j + HD]
            acc = acc + piece * piece
        SS[e, x] = token_rows(acc)
        tp_send_all(2, SS, e, tp_recv.at[1, e % 2])

    loads[0].wait()
    loads[2].wait()
    send_squares(0, X[0].astype(F32))

    def spread(l, carry):
        slot = wbuf.at[l, c, y, z]
        arrived(slot, s1_recv.at[l])

        def go(i, inner):
            remote(slot, slot, sent.at[5], z_recv.at[l], z_peer((z + i) % NZ)).start()
            return inner

        return lax.fori_loop(1, NZ, go, carry)

    lax.fori_loop(0, L, spread, 0)

    def along_y(l):
        arrived(wbuf.at[l, c, y, 0 : NZ - 1], z_recv.at[l])
        slot = wbuf.at[l, c, y]
        for i in (2, 1, 3):
            remote(slot, slot, sent.at[6], y_recv.at[l], y_peer((y + i) % NY)).start()

    def to_core(l):
        arrived(wbuf.at[l, c, 0 : NY - 1], y_recv.at[l])
        slot = wbuf.at[l, c]
        remote(slot, slot, sent.at[7], k_recv.at[l], core_peer).start()

    along_y(0)
    along_y(1)
    to_core(0)

    def w1(l, t):
        return jnp.concatenate(
            [
                wbuf[l, cc, yy, 2 * t + h, 0:16, :]
                for cc in range(2) for h in range(2) for yy in range(NY)
            ],
            axis=0,
        )

    def w2(l, t):
        heads = [
            jnp.concatenate(
                [wbuf[l, cc, yy, 2 * t + h, 16:32, :] for h in range(2) for yy in range(NY)], axis=0
            )
            for cc in range(2)
        ]
        return jnp.concatenate(heads, axis=1)

    def gains(l, t):
        heads = []
        for cc in range(2):
            g8 = wbuf[l, cc, 0, 2 * t, 32:40, :].astype(F32)
            heads.append(jnp.concatenate([g8] * 8, axis=0))
        return jnp.concatenate(heads, axis=1)

    def cols_of(t):
        return slice(256 * t, 256 * t + 256)

    def lanes_of(t):
        return slice(HD * t, HD * t + HD)

    def forward(l, carry):
        arrived(wbuf.at[l, c], k_recv.at[l])
        raw = []
        for t in range(4):
            h = (X[l, :, cols_of(t)].astype(F32) * gains(l, t)).astype(BF16)
            H[l, :, cols_of(t)] = h
            raw.append(dot_nt(h, pair_blocks(h)))
        tp_wait(SS, l, tp_recv.at[1, l % 2])
        f_row = lax.rsqrt(tp_sum(SS, l) * (1.0 / D) + 1e-05)
        Fr[l] = f_row
        f_key = f_row[0:1]
        scale = to_column(f_row) * f_key * (1.0 / HD)
        mask = MK[...]
        part = jnp.zeros((T, HD), F32)
        for t in range(4):
            e = jnp.exp(raw[t] * scale).astype(BF16)
            ES[l, :, lanes_of(t)] = e
            e = (e.astype(F32) * mask).astype(BF16)
            sums = dot(e, ones_blocks)
            prob = (e.astype(F32) * f_key / sums).astype(BF16)
            mixed = dot(prob, pair_blocks(H[l, :, cols_of(t)])).astype(BF16)
            M[l, :, cols_of(t)] = mixed
            part = part + dot(mixed, w1(l, t))
        RR[l, x] = part.astype(BF16)
        tp_send_all(1, RR, l, tp_recv.at[0, l % 2])

        @pl.when(l > 0)
        def _():
            cross = jnp.zeros((T, HD), F32)
            for t in range(4):
                cross = cross + dot_nt(X[l, :, cols_of(t)], w2(l - 1, t))
            BB[l, x] = cross.astype(BF16)
            tp_send_all(3, BB, l, b_recv.at[0])

        @pl.when(l == L - 1)
        def _():
            loads[1].wait()
            loads[3].wait()
            acc = jnp.zeros((T, HD), F32)
            for t in range(4):
                acc = acc + dot_nt(M[L, :, cols_of(t)], w2(L - 1, t))
            AA[L - 1, x, 0:64, :] = acc.astype(BF16)
            AA[L - 1, x, 64:80, :] = jnp.zeros((16, HD), BF16)
            tp_send_all(4, AA, L - 1, tp_recv.at[2, (L - 1) % 2])
            DYP[...] = M[L].astype(F32)

        @pl.when(l + 1 < L)
        def _():
            to_core(l + 1)

        @pl.when(l + 2 < L)
        def _():
            along_y(l + 2)

        tp_wait(RR, l, tp_recv.at[0, l % 2])
        r = tp_sum(RR, l).astype(BF16)
        R[l] = r
        for t in range(4):
            X[l + 1, :, cols_of(t)] = (
                X[l, :, cols_of(t)].astype(F32) + dot(r, w2(l, t))
            ).astype(BF16)

        @pl.when(l < L - 1)
        def _():
            send_squares(l + 1, X[l + 1].astype(F32))

        return carry

    lax.fori_loop(0, L, forward, 0)

    def one_layer(l):
        f_row = Fr[l]
        f_key = f_row[0:1]
        f_col = to_column(f_row)
        mask = MK[...]
        mask_t = MKT[...]
        for t in range(4):
            es = ES[l, :, lanes_of(t)].astype(F32)
            e = es * mask
            sums = dot(e.astype(BF16), ones_blocks)
            PS[:, lanes_of(t)] = e / sums
            et = es * mask_t
            PT[:, lanes_of(t)] = et / jnp.sum(et, axis=0, keepdims=True)

        @pl.when(l == L - 1)
        def _():
            arrived(BB.at[1:L, 0 : NX - 1], b_recv.at[0])

        tp_wait(AA, l, tp_recv.at[2, l % 2])
        total = tp_sum(AA, l)
        s_row = total[64:72] + total[72:80]
        f_next = Fr[l + 1]
        coef = to_column(f_next * f_next * f_next * s_row * (1.0 / D))
        dr = total[:64] - coef * tp_sum(BB, l + 1)
        dr_b = dr.astype(BF16)
        coef2 = twice(coef)
        f_col2 = twice(f_col)
        s_part = jnp.zeros((T, HD), F32)
        acc = jnp.zeros((T, HD), F32)
        below = jnp.maximum(l - 1, 0)
        for t in range(4):
            h = H[l, :, cols_of(t)]
            blocks = pair_blocks(h)
            dm = dot_nt(dr_b, w1(l, t)).astype(BF16)
            dm_blocks = pair_blocks(dm)
            prob = PS[:, lanes_of(t)]
            prob_t = PT[:, lanes_of(t)]
            dp = dot_nt(dm, blocks) * f_key
            dp_t = dot_nt(h, dm_blocks) * f_col
            inner = dot((prob * dp).astype(BF16), ones_blocks)
            ds = prob * (dp - inner)
            inner_t = jnp.sum(prob_t * dp_t, axis=0, keepdims=True)
            ds_t = prob_t * (dp_t - inner_t)
            both = (ds + ds_t) * f_key * (1.0 / HD)
            left = jnp.concatenate((both.astype(BF16), prob_t.astype(BF16)), axis=1)
            dn = dot(left, jnp.concatenate((blocks, dm_blocks), axis=0))
            xs = X[l, :, cols_of(t)].astype(F32)
            gdn = dn * gains(l, t)
            dy = DYP[:, cols_of(t)] - X[l + 1, :, cols_of(t)].astype(F32) * coef2
            M[L, :, cols_of(t)] = dy.astype(BF16)
            dyp = dy + gdn * f_col2
            DYP[:, cols_of(t)] = dyp
            acc = acc + dot_nt(dyp.astype(BF16), w2(below, t))
            prod = gdn * xs
            s_part = s_part + prod[:, :HD] + prod[:, HD:]
            dgain = jnp.sum(dn * xs * f_col2, axis=0, keepdims=True)
            wide = jnp.broadcast_to(dgain, (8, 256)).astype(BF16)
            for cc in range(2):
                for h2 in range(2):
                    for yy in range(NY):
                        G[l, cc, yy, 2 * t + h2, 32:40, :] = wide[:, HD * cc : HD * cc + HD]

        @pl.when(l > 0)
        def _():
            s_new = token_rows(s_part)
            s_high = s_new.astype(BF16).astype(F32)
            AA[below, x, 0:64, :] = acc.astype(BF16)
            AA[below, x, 64:80, :] = jnp.concatenate((s_high, s_new - s_high), axis=0).astype(BF16)
            tp_send_all(4, AA, below, tp_recv.at[2, below % 2])

        zeros = jnp.zeros((T, HD), F32)
        dr_t = jnp.transpose(jnp.concatenate((dr, zeros), axis=0)).astype(BF16)[:, :T]
        r_t = jnp.transpose(jnp.concatenate((R[l].astype(F32), zeros), axis=0)).astype(BF16)[:, :T]
        for t in range(4):
            g1 = dot(dr_t, M[l, :, cols_of(t)]).astype(BF16)
            g2 = dot(r_t, M[L, :, cols_of(t)]).astype(BF16)
            for cc in range(2):
                for q in range(8):
                    rows = slice(64 * (q % 2) + 16 * (q // 2), 64 * (q % 2) + 16 * (q // 2) + 16)
                    lanes = slice(HD * cc, HD * cc + HD)
                    G[l, cc, q // 2, 2 * t + q % 2, 0:16, :] = g1[rows, lanes]
                    G[l, cc, q // 2, 2 * t + q % 2, 16:32, :] = g2[rows, lanes]
        remote(G.at[l, 1 - c], RA.at[l], sent.at[8], ga_recv.at[l], core_peer).start()

    def core_sums(l):
        arrived(RA.at[l], ga_recv.at[l])

        def one(i, carry):
            SA[l, i] = (G[l, c, i].astype(F32) + RA[l, i].astype(F32)).astype(BF16)
            return carry

        lax.fori_loop(0, NY, one, 0)
        RB[l, y] = SA[l, y]
        for i in (2, 1, 3):
            yy = (y + i) % NY
            remote(SA.at[l, yy], RB.at[l, y], sent.at[9], gy_recv.at[l], y_peer(yy)).start()

    def y_sums(l):
        arrived(RB.at[l, 0 : NY - 1], gy_recv.at[l])
        total = RB[l, 0].astype(F32)
        for i in range(1, NY):
            total = total + RB[l, i].astype(F32)
        SB[l] = total.astype(BF16)
        RC[l, z] = SB[l, z]

        def go(i, carry):
            zz = (z + i) % NZ
            remote(SB.at[l, zz], RC.at[l, z], sent.at[10], gz_recv.at[l], z_peer(zz)).start()
            return carry

        lax.fori_loop(1, NZ, go, 0)

    def z_sums(l):
        arrived(RC.at[l, 0 : NZ - 1], gz_recv.at[l])
        total = RC[l, 0].astype(F32)
        for i in range(1, NZ):
            total = total + RC[l, i].astype(F32)
        SD[l] = total.astype(BF16)
        mine = is_me(owner(l))

        @pl.when(mine)
        def _():
            pltpu.make_async_copy(SD.at[l], RD.at[y, z % 2], go_recv.at[0]).start()

        @pl.when(jnp.logical_not(mine))
        def _():
            remote(SD.at[l], RD.at[y, z % 2], sent.at[11], go_recv.at[0], owner(l)).start()

    def backward(i, carry):
        @pl.when(i < L)
        def _():
            one_layer(L - 1 - i)

        @pl.when((i >= 1) & (i < L + 1))
        def _():
            core_sums(L - i)

        @pl.when((i >= 2) & (i < L + 2))
        def _():
            y_sums(L + 1 - i)

        @pl.when(i >= 3)
        def _():
            z_sums(L + 2 - i)

        return carry

    lax.fori_loop(0, L + 3, backward, 0)

    arrived(RD, go_recv.at[0])
    grads = []
    for part in range(2):
        rows = slice(16 * part, 16 * part + 16)
        blocks = [RD[yy, h, rows, :].astype(F32) for h in range(2) for yy in range(NY)]
        grads.append(jnp.concatenate(blocks, axis=0))
    first_out[0] = jnp.transpose(grads[0])
    second_out[0] = grads[1]
    gain_out[...] = RD[0, 0, 32:40, :].astype(F32)[0:1]

    for used, sem, pieces in ((me_holder, 0, chunk), (me_owner, 11, SD)):
        @pl.when(used > 0)
        def _():
            arrived(pieces.at[0:7], sent.at[sem])

        @pl.when(used == 0)
        def _():
            arrived(pieces, sent.at[sem])

    arrived(RR.at[0:6], sent.at[1])
    arrived(SS.at[0:6], sent.at[2])
    arrived(BB.at[0:7, 0:3], sent.at[3])
    arrived(AA.at[0:6], sent.at[4])
    arrived(wbuf.at[0:7, 0, 0], sent.at[5])
    arrived(wbuf.at[0:3], sent.at[6])
    arrived(wbuf.at[0:4], sent.at[7])
    arrived(G.at[0:4], sent.at[8])
    arrived(SA.at[0:6], sent.at[9])
    arrived(SB.at[0:7], sent.at[10])


def per_device(tokens, cotangents, starts, counts, layer_gains, first_map, second_map):
    vmem = pl.BlockSpec(memory_space=pltpu.VMEM)
    smem = pl.BlockSpec(memory_space=pltpu.SMEM)
    hbm = pl.BlockSpec(memory_space=pl.ANY)
    sem = pltpu.SemaphoreType.DMA
    return pl.pallas_call(
        kernel,
        out_shape=(
            jax.ShapeDtypeStruct((1, HD), F32),
            jax.ShapeDtypeStruct((1, HD, HD), F32),
            jax.ShapeDtypeStruct((1, HD, HD), F32),
        ),
        in_specs=[hbm, hbm, smem, smem, hbm, hbm, hbm],
        out_specs=(vmem, vmem, vmem),
        scratch_shapes=[
            pltpu.VMEM((8, PR, HD), BF16),
            pltpu.VMEM((1, HD), BF16),
            pltpu.VMEM((1, HD, HD), BF16),
            pltpu.VMEM((1, HD, HD), BF16),
            pltpu.VMEM((L, 2, NY, NZ, PR, HD), BF16),
            pltpu.VMEM((L + 1, T, C), BF16),
            pltpu.VMEM((L, T, C), BF16),
            pltpu.VMEM((L + 1, T, C), BF16),
            pltpu.VMEM((L, T, 4 * HD), BF16),
            pltpu.VMEM((L + 1, 8, HD), F32),
            pltpu.VMEM((L, T, HD), BF16),
            pltpu.VMEM((L, NX, T, HD), BF16),
            pltpu.VMEM((L, NX, 8, HD), F32),
            pltpu.VMEM((L + 1, NX, T, HD), BF16),
            pltpu.VMEM((L, NX, 80, HD), BF16),
            pltpu.VMEM((T, 4 * HD), F32),
            pltpu.VMEM((T, 4 * HD), F32),
            pltpu.VMEM((T, C), F32),
            pltpu.VMEM((T, HD), F32),
            pltpu.VMEM((T, HD), F32),
            pltpu.VMEM((L, 2, NY, NZ, PR, HD), BF16),
            pltpu.VMEM((L, NY, NZ, PR, HD), BF16),
            pltpu.VMEM((L, NY, NZ, PR, HD), BF16),
            pltpu.VMEM((L, NY, NZ, PR, HD), BF16),
            pltpu.VMEM((L, NZ, PR, HD), BF16),
            pltpu.VMEM((L, NZ, PR, HD), BF16),
            pltpu.VMEM((L, PR, HD), BF16),
            pltpu.VMEM((NY, 2, PR, HD), BF16),
            sem((7,)), sem((12,)),
            sem((L,)), sem((L,)), sem((L,)), sem((L,)),
            sem((3, 2)), sem((1,)),
            sem((L,)), sem((L,)), sem((L,)), sem((1,)),
        ],
        compiler_params=pltpu.CompilerParams(
            collective_id=0, has_side_effects=True, vmem_limit_bytes=VMEM_LIMIT
        ),
    )(tokens, cotangents, starts, counts, layer_gains, first_map, second_map)


def solution(mesh):
    in_specs = (
        P(None, "dp", None, None),
        P(None, "dp", None, None),
        P(None, "dp", None),
        P(None, "dp"),
        P("pipe", "dp"),
        P("pipe", "dp", None),
        P("pipe", None, "dp"),
    )
    out_specs = (P("pipe", "dp"), P("pipe", "dp", None), P("pipe", None, "dp"))
    return jax.shard_map(
        per_device, mesh=mesh, in_specs=in_specs, out_specs=out_specs, check_vma=False
    )
```

time: 212 us -> 158 us (0.75); the launches traced: 208 us -> 157 us
  Pallas kernels: 200 us -> 153 us
  local copies, waits for them, and re-layouts: 7.74 us -> 3.26 us
    pallas_call x1, Pallas kernels: 200 us -> 153 us  [per_device(): pl.pallas_call(kernel, out_shape=(jax.ShapeDtypeStruct((1, HD), F32), jax...]
    unnamed x17 -> x7, local copies, waits for them, and re-layouts: 7.74 us -> 3.26 us
where the time goes in v2:
time: 158 us; the launch traced here: 157 us
  Pallas kernels  153 us (97%)
  local copies, waits for them, and re-layouts  3.26 us (2%)
    pallas_call x1, Pallas kernels, per_device(): pl.pallas_call(kernel, out_shape=(jax.ShapeDtypeStruct((1, HD), F32), jax...  153 us
    unnamed x7, local copies, waits for them, and re-layouts  3.26 us

profile of v2, /device:TPU:64, one launch (start us, length us, event | category | flops | bytes accessed | tf_op | source)
XLA Modules:
  0.0 156.7 jit_solution(4195109921079072839)
XLA Ops:
  0.6 152.7 %shard_map.94 = (f32[1,128]{1,0:T(1,128)}, f32[1,128,128]{2,1,0:T(8,128)}, f32[1,128,128]{2,1,0:T(8,128)}) custom-call(bf16[2,2,32,4096]{3,2,1,0:T(8,128)(2,1)} %tok.1, bf16[2,2,32,4096]{3,2,1,0:T(8,128)(2,1)} %cot.1, s32[2,2,4]{2,1,0:T(2,128)} %starts.1, s32[2,2]{1,0:T(2,128)} %counts.1, bf16[1,128]{1,0:T(2,128)(2,1)} %gain_in.1, ...), custom_call_target="tpu_custom_call" | custom-call | tf_op jit(solution)/shard_map/pallas_call | solution.py:533
  153.4 0.0 copy-start.1
  153.4 0.6 copy-done.1
  154.0 0.5 copy.13
  154.5 0.0 copy-start
  154.5 1.5 copy.14
  156.0 0.0 copy-done
  156.0 0.6 copy.15
Async XLA Ops:
  153.4 0.6 copy-start.1
  154.5 1.5 copy-start

commit v3 on v2

--- a/solution.py
+++ b/solution.py
@@ -53,9 +53,9 @@
 def kernel(
     tok, cot, starts, counts, gain_in, first_in, second_in,
     gain_out, first_out, second_out,
-    chunk, own_gain, own_first, own_second, wbuf, X, H, M, ES, Fr, R, RR, SS, BB, AA,
+    chunk, own_gain, own_first, own_second, wbuf, X, H, M, ES, Fr, R, RR, SS, UU, AA, BS, Q, GP, GX, GF,
     PS, PT, DYP, MK, MKT, G, RA, SA, RB, SB, RC, SD, RD,
-    in_sem, sent, s1_recv, z_recv, y_recv, k_recv, tp_recv, b_recv,
+    in_sem, sent, s1_recv, z_recv, y_recv, y2_recv, k_recv, tp_recv,
     ga_recv, gy_recv, gz_recv, go_recv,
 ):
     p = lax.axis_index("pipe")
@@ -155,11 +155,13 @@
     MK[...] = jnp.where(same & (lane_id <= row_id), 1.0, 0.0)
     MKT[...] = jnp.where(same & (row_id <= lane_id), 1.0, 0.0)
     Fr[L] = jnp.zeros((8, HD), F32)
-    for i in range(NX):
-        BB[L, i] = jnp.zeros((T, HD), BF16)
+    BS[L] = jnp.zeros((T, HD), F32)
     half_r = lax.broadcasted_iota(jnp.int32, (HD, HD), 0) // T
     half_l = lax.broadcasted_iota(jnp.int32, (HD, HD), 1) // T
     ones_blocks = jnp.where(half_r == half_l, 1.0, 0.0).astype(BF16)
+    head_r = lax.broadcasted_iota(jnp.int32, (2 * HD, HD), 0) // HD
+    head_l = lax.broadcasted_iota(jnp.int32, (2 * HD, HD), 1) // T
+    ones_heads = jnp.where(head_r == head_l, 1.0, 0.0).astype(BF16)
 
     me_holder = jnp.int32(0)
     me_owner = jnp.int32(0)
@@ -205,17 +207,14 @@
             total = total + buf[e, i].astype(F32)
         return total
 
-    def send_squares(e, value):
-        acc = jnp.zeros((T, HD), F32)
-        for j in range(C // HD):
-            piece = value[:, HD * j : HD * j + HD]
-            acc = acc + piece * piece
-        SS[e, x] = token_rows(acc)
-        tp_send_all(2, SS, e, tp_recv.at[1, e % 2])
-
     loads[0].wait()
     loads[2].wait()
-    send_squares(0, X[0].astype(F32))
+    acc = jnp.zeros((T, HD), F32)
+    for j in range(C // HD):
+        piece = X[0, :, HD * j : HD * j + HD].astype(F32)
+        acc = acc + piece * piece
+    SS[0, x] = token_rows(acc)
+    tp_send_all(2, SS, 0, tp_recv.at[5, 0])
 
     def spread(l, carry):
         slot = wbuf.at[l, c, y, z]
@@ -232,17 +231,26 @@
     def along_y(l):
         arrived(wbuf.at[l, c, y, 0 : NZ - 1], z_recv.at[l])
         slot = wbuf.at[l, c, y]
-        for i in (2, 1, 3):
+        for i in (1, 3):
             remote(slot, slot, sent.at[6], y_recv.at[l], y_peer((y + i) % NY)).start()
 
+    def along_y_again(l):
+        arrived(wbuf.at[l, c, 0:2], y_recv.at[l])
+        for i, half in ((1, 0), (3, NZ // 2)):
+            slot = wbuf.at[l, c, (y + NY - i) % NY, half : half + NZ // 2]
+            remote(slot, slot, sent.at[12], y2_recv.at[l], y_peer((y + i) % NY)).start()
+
     def to_core(l):
-        arrived(wbuf.at[l, c, 0 : NY - 1], y_recv.at[l])
+        arrived(wbuf.at[l, c, 0], y2_recv.at[l])
         slot = wbuf.at[l, c]
         remote(slot, slot, sent.at[7], k_recv.at[l], core_peer).start()
 
     along_y(0)
+    along_y_again(0)
     along_y(1)
     to_core(0)
+    along_y_again(1)
+    along_y(2)
 
     def w1(l, t):
         return jnp.concatenate(
@@ -275,15 +283,55 @@
     def lanes_of(t):
         return slice(HD * t, HD * t + HD)
 
+    def gram_part(l):
+        total = jnp.zeros((HD, HD), F32)
+        for t in range(4):
+            block = w2(l, t)
+            total = total + dot_nt(block, block)
+        for i in range(NX):
+            GP[l, i] = total[32 * i : 32 * i + 32]
+        GX[l, x] = GP[l, x]
+        for i in (2, 1, 3):
+            dst = (x + i) % NX
+            remote(
+                GP.at[l, dst], GX.at[l, x], sent.at[13], tp_recv.at[3, l % 2], x_peer(i)
+            ).start()
+
+    def gram_sum(l):
+        tp_wait(GX, l, tp_recv.at[3, l % 2])
+        GF[l, x] = tp_sum(GX, l)
+        tp_send_all(14, GF, l, tp_recv.at[4, l % 2])
+
+    arrived(wbuf.at[0, c], k_recv.at[0])
+    gram_part(0)
+
     def forward(l, carry):
-        arrived(wbuf.at[l, c], k_recv.at[l])
         raw = []
         for t in range(4):
             h = (X[l, :, cols_of(t)].astype(F32) * gains(l, t)).astype(BF16)
             H[l, :, cols_of(t)] = h
             raw.append(dot_nt(h, pair_blocks(h)))
-        tp_wait(SS, l, tp_recv.at[1, l % 2])
-        f_row = lax.rsqrt(tp_sum(SS, l) * (1.0 / D) + 1e-05)
+
+        @pl.when(l == 0)
+        def _():
+            tp_wait(SS, 0, tp_recv.at[5, 0])
+            Q[...] = tp_sum(SS, 0)
+
+        @pl.when(l > 0)
+        def _():
+            below = jnp.maximum(l - 1, 0)
+            tp_wait(UU, below, tp_recv.at[1, below % 2])
+            tp_wait(GF, below, tp_recv.at[4, below % 2])
+            gram = GF[below].reshape(HD, HD)
+            high = gram.astype(BF16)
+            low = (gram - high.astype(F32)).astype(BF16)
+            r = R[below]
+            u = tp_sum(UU, below)
+            rg = dot(jnp.concatenate((r, r), axis=1), jnp.concatenate((high, low), axis=0))
+            BS[l] = u + rg
+            Q[...] = Q[...] + token_rows(r.astype(F32) * (2.0 * u + rg))
+
+        f_row = lax.rsqrt(jnp.maximum(Q[...], 0.0) * (1.0 / D) + 1e-05)
         Fr[l] = f_row
         f_key = f_row[0:1]
         scale = to_column(f_row) * f_key * (1.0 / HD)
@@ -301,13 +349,13 @@
         RR[l, x] = part.astype(BF16)
         tp_send_all(1, RR, l, tp_recv.at[0, l % 2])
 
-        @pl.when(l > 0)
-        def _():
-            cross = jnp.zeros((T, HD), F32)
+        @pl.when(l < L - 1)
+        def _():
+            u = jnp.zeros((T, HD), F32)
             for t in range(4):
-                cross = cross + dot_nt(X[l, :, cols_of(t)], w2(l - 1, t))
-            BB[l, x] = cross.astype(BF16)
-            tp_send_all(3, BB, l, b_recv.at[0])
+                u = u + dot_nt(X[l, :, cols_of(t)], w2(l, t))
+            UU[l, x] = u.astype(BF16)
+            tp_send_all(3, UU, l, tp_recv.at[1, l % 2])
 
         @pl.when(l == L - 1)
         def _():
@@ -325,9 +373,25 @@
         def _():
             to_core(l + 1)
 
+        @pl.when(l < L - 1)
+        def _():
+            gram_sum(l)
+
         @pl.when(l + 2 < L)
         def _():
-            along_y(l + 2)
+            along_y_again(l + 2)
+
+        @pl.when(l + 3 < L)
+        def _():
+            along_y(l + 3)
+
+        @pl.when(l + 1 < L)
+        def _():
+            arrived(wbuf.at[l + 1, c], k_recv.at[l + 1])
+
+        @pl.when(l + 1 < L - 1)
+        def _():
+            gram_part(l + 1)
 
         tp_wait(RR, l, tp_recv.at[0, l % 2])
         r = tp_sum(RR, l).astype(BF16)
@@ -336,10 +400,6 @@
             X[l + 1, :, cols_of(t)] = (
                 X[l, :, cols_of(t)].astype(F32) + dot(r, w2(l, t))
             ).astype(BF16)
-
-        @pl.when(l < L - 1)
-        def _():
-            send_squares(l + 1, X[l + 1].astype(F32))
 
         return carry
 
@@ -359,16 +419,12 @@
             et = es * mask_t
             PT[:, lanes_of(t)] = et / jnp.sum(et, axis=0, keepdims=True)
 
-        @pl.when(l == L - 1)
-        def _():
-            arrived(BB.at[1:L, 0 : NX - 1], b_recv.at[0])
-
         tp_wait(AA, l, tp_recv.at[2, l % 2])
         total = tp_sum(AA, l)
         s_row = total[64:72] + total[72:80]
         f_next = Fr[l + 1]
         coef = to_column(f_next * f_next * f_next * s_row * (1.0 / D))
-        dr = total[:64] - coef * tp_sum(BB, l + 1)
+        dr = total[:64] - coef * BS[l + 1]
         dr_b = dr.astype(BF16)
         coef2 = twice(coef)
         f_col2 = twice(f_col)
@@ -382,9 +438,9 @@
             dm_blocks = pair_blocks(dm)
             prob = PS[:, lanes_of(t)]
             prob_t = PT[:, lanes_of(t)]
+            inner = dot(dm * M[l, :, cols_of(t)], ones_heads)
             dp = dot_nt(dm, blocks) * f_key
             dp_t = dot_nt(h, dm_blocks) * f_col
-            inner = dot((prob * dp).astype(BF16), ones_blocks)
             ds = prob * (dp - inner)
             inner_t = jnp.sum(prob_t * dp_t, axis=0, keepdims=True)
             ds_t = prob_t * (dp_t - inner_t)
@@ -514,11 +570,14 @@
             arrived(pieces, sent.at[sem])
 
     arrived(RR.at[0:6], sent.at[1])
-    arrived(SS.at[0:6], sent.at[2])
-    arrived(BB.at[0:7, 0:3], sent.at[3])
+    arrived(SS.at[0, 0:3], sent.at[2])
+    arrived(UU.at[0:7, 0:3], sent.at[3])
     arrived(AA.at[0:6], sent.at[4])
     arrived(wbuf.at[0:7, 0, 0], sent.at[5])
-    arrived(wbuf.at[0:3], sent.at[6])
+    arrived(wbuf.at[0:2], sent.at[6])
+    arrived(wbuf.at[0:1], sent.at[12])
+    arrived(GP.at[0:7, 0:3], sent.at[13])
+    arrived(GF.at[0:7, 0:3], sent.at[14])
     arrived(wbuf.at[0:4], sent.at[7])
     arrived(G.at[0:4], sent.at[8])
     arrived(SA.at[0:6], sent.at[9])
@@ -552,9 +611,14 @@
             pltpu.VMEM((L + 1, 8, HD), F32),
             pltpu.VMEM((L, T, HD), BF16),
             pltpu.VMEM((L, NX, T, HD), BF16),
-            pltpu.VMEM((L, NX, 8, HD), F32),
-            pltpu.VMEM((L + 1, NX, T, HD), BF16),
+            pltpu.VMEM((1, NX, 8, HD), F32),
+            pltpu.VMEM((L, NX, T, HD), BF16),
             pltpu.VMEM((L, NX, 80, HD), BF16),
+            pltpu.VMEM((L + 1, T, HD), F32),
+            pltpu.VMEM((8, HD), F32),
+            pltpu.VMEM((L, NX, HD // NX, HD), F32),
+            pltpu.VMEM((L, NX, HD // NX, HD), F32),
+            pltpu.VMEM((L, NX, HD // NX, HD), F32),
             pltpu.VMEM((T, 4 * HD), F32),
             pltpu.VMEM((T, 4 * HD), F32),
             pltpu.VMEM((T, C), F32),
@@ -568,9 +632,9 @@
             pltpu.VMEM((L, NZ, PR, HD), BF16),
             pltpu.VMEM((L, PR, HD), BF16),
             pltpu.VMEM((NY, 2, PR, HD), BF16),
-            sem((7,)), sem((12,)),
-            sem((L,)), sem((L,)), sem((L,)), sem((L,)),
-            sem((3, 2)), sem((1,)),
+            sem((7,)), sem((15,)),
+            sem((L,)), sem((L,)), sem((L,)), sem((L,)), sem((L,)),
+            sem((6, 2)),
             sem((L,)), sem((L,)), sem((L,)), sem((1,)),
         ],
         compiler_params=pltpu.CompilerParams(

time: 158 us -> 143 us (0.905)
  Pallas kernels: 153 us -> 139 us
    pallas_call x1, Pallas kernels: 153 us -> 139 us  [per_device(): pl.pallas_call(kernel, out_shape=(jax.ShapeDtypeStruct((1, HD), F32), jax...]
where the time goes in v3:
time: 143 us
  Pallas kernels  139 us (97%)
  local copies, waits for them, and re-layouts  3.26 us (2%)
    pallas_call x1, Pallas kernels, per_device(): pl.pallas_call(kernel, out_shape=(jax.ShapeDtypeStruct((1, HD), F32), jax...  139 us
    unnamed x7, local copies, waits for them, and re-layouts  3.26 us

profile of v3, /device:TPU:64, one launch (start us, length us, event | category | flops | bytes accessed | tf_op | source)
XLA Modules:
  0.0 143.1 jit_solution(8685355246227898433)
XLA Ops:
  0.6 139.2 %shard_map.94 = (f32[1,128]{1,0:T(1,128)}, f32[1,128,128]{2,1,0:T(8,128)}, f32[1,128,128]{2,1,0:T(8,128)}) custom-call(bf16[2,2,32,4096]{3,2,1,0:T(8,128)(2,1)} %tok.1, bf16[2,2,32,4096]{3,2,1,0:T(8,128)(2,1)} %cot.1, s32[2,2,4]{2,1,0:T(2,128)} %starts.1, s32[2,2]{1,0:T(2,128)} %counts.1, bf16[1,128]{1,0:T(2,128)(2,1)} %gain_in.1, ...), custom_call_target="tpu_custom_call" | custom-call | tf_op jit(solution)/shard_map/pallas_call | solution.py:592
  139.8 0.0 copy-start.1
  139.8 0.6 copy-done.1
  140.4 0.5 copy.13
  140.9 0.0 copy-start
  140.9 1.5 %copy.14 = f32[1,128,128]{2,1,0:T(8,128)} copy(f32[1,128,128]{2,1,0:T(8,128)} %get-tuple-element.7) | data formatting | bytes 131072
  142.5 0.0 copy-done
  142.5 0.6 copy.15
Async XLA Ops:
  139.8 0.6 copy-start.1
  140.9 1.5 %copy-start = (f32[1,128,128]{2,1,0:T(8,128)S(1)}, f32[1,128,128]{2,1,0:T(8,128)}, u32[]{:S(2)}) copy-start(f32[1,128,128]{2,1,0:T(8,128)} %get-tuple-element.8) | copy-start | bytes 196612

commit v4 on v3

--- a/solution.py
+++ b/solution.py
@@ -54,7 +54,7 @@
     tok, cot, starts, counts, gain_in, first_in, second_in,
     gain_out, first_out, second_out,
     chunk, own_gain, own_first, own_second, wbuf, X, H, M, ES, Fr, R, RR, SS, UU, AA, BS, Q, GP, GX, GF,
-    PS, PT, DYP, MK, MKT, G, RA, SA, RB, SB, RC, SD, RD,
+    PS, PT, ZS, YS, DYP, MK, MKT, G, RA, SA, RB, SB, RC, SD, RD,
     in_sem, sent, s1_recv, z_recv, y_recv, y2_recv, k_recv, tp_recv,
     ga_recv, gy_recv, gz_recv, go_recv,
 ):
@@ -159,6 +159,9 @@
     half_r = lax.broadcasted_iota(jnp.int32, (HD, HD), 0) // T
     half_l = lax.broadcasted_iota(jnp.int32, (HD, HD), 1) // T
     ones_blocks = jnp.where(half_r == half_l, 1.0, 0.0).astype(BF16)
+    wide_r = lax.broadcasted_iota(jnp.int32, (HD, 2 * HD), 0) // T
+    wide_l = lax.broadcasted_iota(jnp.int32, (HD, 2 * HD), 1) // HD
+    ones_wide = jnp.where(wide_r == wide_l, 1.0, 0.0).astype(BF16)
     head_r = lax.broadcasted_iota(jnp.int32, (2 * HD, HD), 0) // HD
     head_l = lax.broadcasted_iota(jnp.int32, (2 * HD, HD), 1) // T
     ones_heads = jnp.where(head_r == head_l, 1.0, 0.0).astype(BF16)
@@ -246,11 +249,14 @@
         remote(slot, slot, sent.at[7], k_recv.at[l], core_peer).start()
 
     along_y(0)
+    along_y(1)
     along_y_again(0)
-    along_y(1)
+    along_y(2)
+    along_y_again(1)
     to_core(0)
-    along_y_again(1)
-    along_y(2)
+    along_y(3)
+    along_y_again(2)
+    to_core(1)
 
     def w1(l, t):
         return jnp.concatenate(
@@ -312,6 +318,14 @@
             H[l, :, cols_of(t)] = h
             raw.append(dot_nt(h, pair_blocks(h)))
 
+        @pl.when(l < L - 1)
+        def _():
+            u = jnp.zeros((T, HD), F32)
+            for t in range(4):
+                u = u + dot_nt(X[l, :, cols_of(t)], w2(l, t))
+            UU[l, x] = u.astype(BF16)
+            tp_send_all(3, UU, l, tp_recv.at[1, l % 2])
+
         @pl.when(l == 0)
         def _():
             tp_wait(SS, 0, tp_recv.at[5, 0])
@@ -341,21 +355,13 @@
             e = jnp.exp(raw[t] * scale).astype(BF16)
             ES[l, :, lanes_of(t)] = e
             e = (e.astype(F32) * mask).astype(BF16)
-            sums = dot(e, ones_blocks)
-            prob = (e.astype(F32) * f_key / sums).astype(BF16)
-            mixed = dot(prob, pair_blocks(H[l, :, cols_of(t)])).astype(BF16)
+            sums = dot(e, ones_wide)
+            weighted = dot((e.astype(F32) * f_key).astype(BF16), pair_blocks(H[l, :, cols_of(t)]))
+            mixed = (weighted / sums).astype(BF16)
             M[l, :, cols_of(t)] = mixed
             part = part + dot(mixed, w1(l, t))
         RR[l, x] = part.astype(BF16)
         tp_send_all(1, RR, l, tp_recv.at[0, l % 2])
-
-        @pl.when(l < L - 1)
-        def _():
-            u = jnp.zeros((T, HD), F32)
-            for t in range(4):
-                u = u + dot_nt(X[l, :, cols_of(t)], w2(l, t))
-            UU[l, x] = u.astype(BF16)
-            tp_send_all(3, UU, l, tp_recv.at[1, l % 2])
 
         @pl.when(l == L - 1)
         def _():
@@ -369,21 +375,21 @@
             tp_send_all(4, AA, L - 1, tp_recv.at[2, (L - 1) % 2])
             DYP[...] = M[L].astype(F32)
 
-        @pl.when(l + 1 < L)
-        def _():
-            to_core(l + 1)
-
         @pl.when(l < L - 1)
         def _():
             gram_sum(l)
 
         @pl.when(l + 2 < L)
         def _():
-            along_y_again(l + 2)
+            to_core(l + 2)
 
         @pl.when(l + 3 < L)
         def _():
-            along_y(l + 3)
+            along_y_again(l + 3)
+
+        @pl.when(l + 4 < L)
+        def _():
+            along_y(l + 4)
 
         @pl.when(l + 1 < L)
         def _():
@@ -418,6 +424,13 @@
             PS[:, lanes_of(t)] = e / sums
             et = es * mask_t
             PT[:, lanes_of(t)] = et / jnp.sum(et, axis=0, keepdims=True)
+            weight = w1(l, t)
+            for src, dst in ((H, ZS), (M, YS)):
+                pair = src[l, :, cols_of(t)]
+                products = [
+                    dot(pair[:, :HD], weight[:HD]), dot(pair[:, HD:], weight[HD:])
+                ]
+                dst[:, cols_of(t)] = jnp.concatenate(products, axis=1).astype(BF16)
 
         tp_wait(AA, l, tp_recv.at[2, l % 2])
         total = tp_sum(AA, l)
@@ -426,6 +439,8 @@
         coef = to_column(f_next * f_next * f_next * s_row * (1.0 / D))
         dr = total[:64] - coef * BS[l + 1]
         dr_b = dr.astype(BF16)
+        dr_blocks = pair_blocks(twice(dr_b))
+        dr2 = twice(dr)
         coef2 = twice(coef)
         f_col2 = twice(f_col)
         s_part = jnp.zeros((T, HD), F32)
@@ -438,9 +453,10 @@
             dm_blocks = pair_blocks(dm)
             prob = PS[:, lanes_of(t)]
             prob_t = PT[:, lanes_of(t)]
-            inner = dot(dm * M[l, :, cols_of(t)], ones_heads)
-            dp = dot_nt(dm, blocks) * f_key
-            dp_t = dot_nt(h, dm_blocks) * f_col
+            zs = ZS[:, cols_of(t)]
+            inner = dot((dr2 * YS[:, cols_of(t)].astype(F32)).astype(BF16), ones_heads)
+            dp = dot_nt(dr_b, jnp.concatenate((zs[:, :HD], zs[:, HD:]), axis=0)) * f_key
+            dp_t = dot_nt(zs, dr_blocks) * f_col
             ds = prob * (dp - inner)
             inner_t = jnp.sum(prob_t * dp_t, axis=0, keepdims=True)
             ds_t = prob_t * (dp_t - inner_t)
@@ -587,7 +603,7 @@
 def per_device(tokens, cotangents, starts, counts, layer_gains, first_map, second_map):
     vmem = pl.BlockSpec(memory_space=pltpu.VMEM)
     smem = pl.BlockSpec(memory_space=pltpu.SMEM)
-    hbm = pl.BlockSpec(memory_space=pl.ANY)
+    hbm = pl.BlockSpec(memory_space=pltpu.HBM)
     sem = pltpu.SemaphoreType.DMA
     return pl.pallas_call(
         kernel,
@@ -621,6 +637,8 @@
             pltpu.VMEM((L, NX, HD // NX, HD), F32),
             pltpu.VMEM((T, 4 * HD), F32),
             pltpu.VMEM((T, 4 * HD), F32),
+            pltpu.VMEM((T, C), BF16),
+            pltpu.VMEM((T, C), BF16),
             pltpu.VMEM((T, C), F32),
             pltpu.VMEM((T, HD), F32),
             pltpu.VMEM((T, HD), F32),

time: 143 us -> 141 us (0.986)
  Pallas kernels: 139 us -> 137 us
    pallas_call x1, Pallas kernels: 139 us -> 137 us  [per_device(): pl.pallas_call(kernel, out_shape=(jax.ShapeDtypeStruct((1, HD), F32), jax...]
where the time goes in v4:
time: 141 us
  Pallas kernels  137 us (97%)
  local copies, waits for them, and re-layouts  3.26 us (2%)
    pallas_call x1, Pallas kernels, per_device(): pl.pallas_call(kernel, out_shape=(jax.ShapeDtypeStruct((1, HD), F32), jax...  137 us
    unnamed x7, local copies, waits for them, and re-layouts  3.26 us

profile of v4, /device:TPU:64, one launch (start us, length us, event | category | flops | bytes accessed | tf_op | source)
XLA Modules:
  0.0 141.3 jit_solution(1527123356677005492)
XLA Ops:
  0.6 137.3 %shard_map.94 = (f32[1,128]{1,0:T(1,128)}, f32[1,128,128]{2,1,0:T(8,128)}, f32[1,128,128]{2,1,0:T(8,128)}) custom-call(bf16[2,2,32,4096]{3,2,1,0:T(8,128)(2,1)} %tok.1, bf16[2,2,32,4096]{3,2,1,0:T(8,128)(2,1)} %cot.1, s32[2,2,4]{2,1,0:T(2,128)} %starts.1, s32[2,2]{1,0:T(2,128)} %counts.1, bf16[1,128]{1,0:T(2,128)(2,1)} %gain_in.1, ...), custom_call_target="tpu_custom_call" | custom-call | tf_op jit(solution)/shard_map/pallas_call | solution.py:608
  138.0 0.0 copy-start.1
  138.0 0.6 copy-done.1
  138.6 0.5 copy.13
  139.1 0.0 copy-start
  139.1 1.5 %copy.14 = f32[1,128,128]{2,1,0:T(8,128)} copy(f32[1,128,128]{2,1,0:T(8,128)} %get-tuple-element.7) | data formatting | bytes 131072
  140.6 0.0 copy-done
  140.6 0.6 copy.15
Async XLA Ops:
  138.0 0.6 copy-start.1
  139.1 1.5 %copy-start = (f32[1,128,128]{2,1,0:T(8,128)S(1)}, f32[1,128,128]{2,1,0:T(8,128)}, u32[]{:S(2)}) copy-start(f32[1,128,128]{2,1,0:T(8,128)} %get-tuple-element.8) | copy-start | bytes 196612

commit v5 on v4

--- a/solution.py
+++ b/solution.py
@@ -156,6 +156,7 @@
     MKT[...] = jnp.where(same & (row_id <= lane_id), 1.0, 0.0)
     Fr[L] = jnp.zeros((8, HD), F32)
     BS[L] = jnp.zeros((T, HD), F32)
+    X[L] = jnp.zeros((T, C), BF16)
     half_r = lax.broadcasted_iota(jnp.int32, (HD, HD), 0) // T
     half_l = lax.broadcasted_iota(jnp.int32, (HD, HD), 1) // T
     ones_blocks = jnp.where(half_r == half_l, 1.0, 0.0).astype(BF16)
@@ -402,10 +403,13 @@
         tp_wait(RR, l, tp_recv.at[0, l % 2])
         r = tp_sum(RR, l).astype(BF16)
         R[l] = r
-        for t in range(4):
-            X[l + 1, :, cols_of(t)] = (
-                X[l, :, cols_of(t)].astype(F32) + dot(r, w2(l, t))
-            ).astype(BF16)
+
+        @pl.when(l < L - 1)
+        def _():
+            for t in range(4):
+                X[l + 1, :, cols_of(t)] = (
+                    X[l, :, cols_of(t)].astype(F32) + dot(r, w2(l, t))
+                ).astype(BF16)
 
         return carry
 
@@ -554,17 +558,17 @@
         def _():
             core_sums(L - i)
 
-        @pl.when((i >= 2) & (i < L + 2))
-        def _():
-            y_sums(L + 1 - i)
-
-        @pl.when(i >= 3)
-        def _():
-            z_sums(L + 2 - i)
+        @pl.when((i >= 3) & (i < L + 3))
+        def _():
+            y_sums(L + 2 - i)
+
+        @pl.when(i >= 4)
+        def _():
+            z_sums(L + 3 - i)
 
         return carry
 
-    lax.fori_loop(0, L + 3, backward, 0)
+    lax.fori_loop(0, L + 4, backward, 0)
 
     arrived(RD, go_recv.at[0])
     grads = []

time: 141 us -> 142 us (level)
  no operation moved by 1% of the time
where the time goes in v5:
time: 142 us; the launch traced here: 141 us
  Pallas kernels  137 us (96%)
  local copies, waits for them, and re-layouts  3.26 us (2%)
    pallas_call x1, Pallas kernels, per_device(): pl.pallas_call(kernel, out_shape=(jax.ShapeDtypeStruct((1, HD), F32), jax...  137 us
    unnamed x7, local copies, waits for them, and re-layouts  3.26 us

profile of v5, /device:TPU:64, one launch (start us, length us, event | category | flops | bytes accessed | tf_op | source)
XLA Modules:
  0.0 141.2 jit_solution(5023187623021163109)
XLA Ops:
  0.6 137.3 %shard_map.94 = (f32[1,128]{1,0:T(1,128)}, f32[1,128,128]{2,1,0:T(8,128)}, f32[1,128,128]{2,1,0:T(8,128)}) custom-call(bf16[2,2,32,4096]{3,2,1,0:T(8,128)(2,1)} %tok.1, bf16[2,2,32,4096]{3,2,1,0:T(8,128)(2,1)} %cot.1, s32[2,2,4]{2,1,0:T(2,128)} %starts.1, s32[2,2]{1,0:T(2,128)} %counts.1, bf16[1,128]{1,0:T(2,128)(2,1)} %gain_in.1, ...), custom_call_target="tpu_custom_call" | custom-call | tf_op jit(solution)/shard_map/pallas_call | solution.py:612
  138.0 0.0 copy-start.1
  138.0 0.6 copy-done.1
  138.6 0.5 copy.13
  139.1 0.0 copy-start
  139.1 1.5 %copy.14 = f32[1,128,128]{2,1,0:T(8,128)} copy(f32[1,128,128]{2,1,0:T(8,128)} %get-tuple-element.7) | data formatting | bytes 131072
  140.6 0.0 copy-done
  140.6 0.6 copy.15
Async XLA Ops:
  138.0 0.6 copy-start.1
  139.1 1.5 %copy-start = (f32[1,128,128]{2,1,0:T(8,128)S(1)}, f32[1,128,128]{2,1,0:T(8,128)}, u32[]{:S(2)}) copy-start(f32[1,128,128]{2,1,0:T(8,128)} %get-tuple-element.8) | copy-start | bytes 196612

commit v6 on v5

--- a/solution.py
+++ b/solution.py
@@ -372,7 +372,7 @@
             for t in range(4):
                 acc = acc + dot_nt(M[L, :, cols_of(t)], w2(L - 1, t))
             AA[L - 1, x, 0:64, :] = acc.astype(BF16)
-            AA[L - 1, x, 64:80, :] = jnp.zeros((16, HD), BF16)
+            AA[L - 1, x, 64:72, :] = jnp.zeros((8, HD), BF16)
             tp_send_all(4, AA, L - 1, tp_recv.at[2, (L - 1) % 2])
             DYP[...] = M[L].astype(F32)
 
@@ -438,7 +438,7 @@
 
         tp_wait(AA, l, tp_recv.at[2, l % 2])
         total = tp_sum(AA, l)
-        s_row = total[64:72] + total[72:80]
+        s_row = total[64:72]
         f_next = Fr[l + 1]
         coef = to_column(f_next * f_next * f_next * s_row * (1.0 / D))
         dr = total[:64] - coef * BS[l + 1]
@@ -486,9 +486,8 @@
         @pl.when(l > 0)
         def _():
             s_new = token_rows(s_part)
-            s_high = s_new.astype(BF16).astype(F32)
             AA[below, x, 0:64, :] = acc.astype(BF16)
-            AA[below, x, 64:80, :] = jnp.concatenate((s_high, s_new - s_high), axis=0).astype(BF16)
+            AA[below, x, 64:72, :] = s_new.astype(BF16)
             tp_send_all(4, AA, below, tp_recv.at[2, below % 2])
 
         zeros = jnp.zeros((T, HD), F32)
@@ -633,7 +632,7 @@
             pltpu.VMEM((L, NX, T, HD), BF16),
             pltpu.VMEM((1, NX, 8, HD), F32),
             pltpu.VMEM((L, NX, T, HD), BF16),
-            pltpu.VMEM((L, NX, 80, HD), BF16),
+            pltpu.VMEM((L, NX, 72, HD), BF16),
             pltpu.VMEM((L + 1, T, HD), F32),
             pltpu.VMEM((8, HD), F32),
             pltpu.VMEM((L, NX, HD // NX, HD), F32),

time: 142 us -> 141 us (level)
  no operation moved by 1% of the time
where the time goes in v6:
time: 141 us
  Pallas kernels  137 us (97%)
  local copies, waits for them, and re-layouts  3.26 us (2%)
    pallas_call x1, Pallas kernels, per_device(): pl.pallas_call(kernel, out_shape=(jax.ShapeDtypeStruct((1, HD), F32), jax...  137 us
    unnamed x7, local copies, waits for them, and re-layouts  3.26 us

profile of v6, /device:TPU:64, one launch (start us, length us, event | category | flops | bytes accessed | tf_op | source)
XLA Modules:
  0.0 140.8 jit_solution(14154429006029549183)
XLA Ops:
  0.6 136.9 %shard_map.94 = (f32[1,128]{1,0:T(1,128)}, f32[1,128,128]{2,1,0:T(8,128)}, f32[1,128,128]{2,1,0:T(8,128)}) custom-call(bf16[2,2,32,4096]{3,2,1,0:T(8,128)(2,1)} %tok.1, bf16[2,2,32,4096]{3,2,1,0:T(8,128)(2,1)} %cot.1, s32[2,2,4]{2,1,0:T(2,128)} %starts.1, s32[2,2]{1,0:T(2,128)} %counts.1, bf16[1,128]{1,0:T(2,128)(2,1)} %gain_in.1, ...), custom_call_target="tpu_custom_call" | custom-call | tf_op jit(solution)/shard_map/pallas_call | solution.py:611
  137.6 0.0 copy-start.1
  137.6 0.6 copy-done.1
  138.2 0.5 copy.13
  138.7 0.0 copy-start
  138.7 1.5 %copy.14 = f32[1,128,128]{2,1,0:T(8,128)} copy(f32[1,128,128]{2,1,0:T(8,128)} %get-tuple-element.7) | data formatting | bytes 131072
  140.2 0.0 copy-done
  140.2 0.6 copy.15
Async XLA Ops:
  137.6 0.6 copy-start.1
  138.7 1.5 %copy-start = (f32[1,128,128]{2,1,0:T(8,128)S(1)}, f32[1,128,128]{2,1,0:T(8,128)}, u32[]{:S(2)}) copy-start(f32[1,128,128]{2,1,0:T(8,128)} %get-tuple-element.8) | copy-start | bytes 196612
